TPU v7x, 128 devices: a whole 4x4x4 slice. The times are simulated.
128 devices in a mesh: seq: 32 (over y, x, core), tp: 4 (over z).
Axes of the slice: x: 4, y: 4, z: 4, core: 2. Of those that a mesh axis runs over, the one named last changes fastest.
Arguments:
- codes: bfloat16 [16384, 4096], P('seq', 'tp'), may hold values from -127 to 127, as said below
- exponents: int32 [16384], P('seq'), may hold values from -8 to -5
- w_query: bfloat16 [4096, 4096], P(None, 'tp'), may hold values from -0.09375 to 0.09375
- w_key: bfloat16 [4096, 4096], P(None, 'tp'), may hold values from -0.09375 to 0.09375
- w_value: bfloat16 [4096, 4096], P(None, 'tp'), may hold values from -0.09375 to 0.09375
- norm_gain: float32 [4096], P('tp'), may hold values from 0.1 to 1.9
- w_out: bfloat16 [4096, 4096], P('tp'), may hold values from -0.09375 to 0.09375
Outputs:
- mixed: bfloat16 [16384, 4096], P(('seq', 'tp'))
Inputs may be any that keep to these rules, and one draw needn't show every extreme that they name: `codes`: every entry is a whole number.
All inputs are finite; a program needn't handle non-finite values.
Results may differ from a plain program's by a relative error of at most 0.012.
Values may be sent and summed in bfloat16 or wider, within the bound.
No kernel may reach another device: no remote copies, remote signals or barrier semaphores. Data moves between devices by JAX's collectives and lax.ppermute only.
A program may use at most 128 MiB of HBM per device.

v0:
```python
import jax
import jax.numpy as jnp
from jax import lax
from jax.sharding import PartitionSpec as P

HD = 128
BLK = 512


def prefix(x, axis, combine, identity):
    length, place = (lax.axis_size(axis), lax.axis_index(axis))
    everything = lax.all_gather(x, axis)
    start = jnp.broadcast_to(jnp.asarray(identity, x.dtype), x.shape)

    def step(k, before):
        reached = k < place
        new = combine(before, everything[k])
        return jnp.where(reached, new, before)

    return lax.fori_loop(0, length, step, start)


def on_device(codes, exponents, w_query, w_key, w_value, norm_gain, w_out):
    tok_count = codes.shape[0]
    local_width = w_query.shape[1]
    heads_local = local_width // HD
    blocks = tok_count // BLK
    row_scale = jnp.exp2(exponents.astype(jnp.float32))[:, None]
    weights = (w_query, w_key, w_value)
    piece = lax.all_gather(codes, "tp", axis=1, tiled=True)
    query, keys, values = tuple(
        (jnp.dot(piece, weight, preferred_element_type=jnp.float32) for weight in weights)
    )
    feat_q = (
        (jax.nn.elu(query * row_scale) + 1.0)
        .astype(jnp.bfloat16)
        .reshape(blocks, BLK, heads_local, HD)
    )
    feat_k = (
        (jax.nn.elu(keys * row_scale) + 1.0)
        .astype(jnp.bfloat16)
        .reshape(blocks, BLK, heads_local, HD)
    )
    value_b = (values * row_scale).astype(jnp.bfloat16).reshape(blocks, BLK, heads_local, HD)
    block_states = jnp.einsum(
        "bshd,bshe->bhde", feat_k, value_b, preferred_element_type=jnp.float32
    )
    shard_state = jnp.sum(block_states, axis=0)
    zero_state = jnp.zeros((heads_local, HD, HD), jnp.float32)
    before = prefix(shard_state, "seq", lambda earlier, later: earlier + later, zero_state)
    states = (before[None] + (jnp.cumsum(block_states, axis=0) - block_states)).astype(jnp.bfloat16)
    inter = jnp.einsum("bshd,bhde->bshe", feat_q, states, preferred_element_type=jnp.float32)
    causal = jnp.tril(jnp.ones((BLK, BLK), jnp.float32))
    scores = jnp.einsum("bshd,bthd->bhst", feat_q, feat_k, preferred_element_type=jnp.float32)
    scores = (scores * causal[None, None]).astype(jnp.bfloat16)
    intra = jnp.einsum("bhst,bthe->bshe", scores, value_b, preferred_element_type=jnp.float32)
    summed = inter + intra
    mean_sq = jnp.mean(summed * summed, axis=-1, keepdims=True)
    gain = norm_gain.reshape(heads_local, HD)
    normed = (
        (summed * lax.rsqrt(mean_sq + 1e-05) * gain)
        .astype(jnp.bfloat16)
        .reshape(tok_count, local_width)
    )
    return lax.psum_scatter(
        jnp.dot(normed, w_out, preferred_element_type=jnp.float32).astype(jnp.bfloat16),
        "tp",
        scatter_dimension=0,
        tiled=True,
    )


def solution(mesh):
    in_specs = (
        P("seq", "tp"),
        P("seq"),
        P(None, "tp"),
        P(None, "tp"),
        P(None, "tp"),
        P("tp"),
        P("tp", None),
    )
    out_specs = P(("seq", "tp"), None)
    return jax.shard_map(
        on_device, mesh=mesh, in_specs=in_specs, out_specs=out_specs, check_vma=False
    )
```

profile of v0, /device:TPU:1, one launch (start us, length us, event | category | flops | bytes accessed | tf_op | source)
XLA Modules:
  0.0 268.6 jit_solution(1697507522976406608)
XLA Ops:
  8.0 52.5 %all-gather.4.cloned.1.call-done = bf16[512,4096]{1,0:T(8,128)(2,1)} async-done(((bf16[512,1024]{1,0:T(8,128)(2,1)}), bf16[512,4096]{1,0:T(8,128)(2,1)}) %all-gather.4.cloned.1.call-update) | async-done | bytes 4194320 | tf_op jit(solution)/shard_map/all_gather | solution.py:30
  60.5 9.8 %fusion.6 = bf16[512,1024]{1,0:T(8,128)(2,1)S(1)} fusion(bf16[512,4096]{1,0:T(8,128)(2,1)} %all-gather.4.cloned.1.call-done, bf16[4096,1024]{1,0:T(8,128)(2,1)} %param.12, f32[512]{0:T(512)S(1)} %multiply_exponential_fusion), kind=kOutput, calls=%fused_computation.12 | convolution fusion | flops 4298113024 | bytes 13633536 | tf_op jit(solution)/shard_map/dot_general | solution.py:32
  70.9 9.1 %multiply_convert_fusion.2 = bf16[512,1024]{1,0:T(8,128)(2,1)S(1)} fusion(bf16[512,4096]{1,0:T(8,128)(2,1)} %all-gather.4.cloned.1.call-done, bf16[4096,1024]{1,0:T(8,128)(2,1)} %param.13, f32[512]{0:T(512)S(1)} %multiply_exponential_fusion), kind=kOutput, calls=%fused_computation.21 | convolution fusion | flops 4296015872 | bytes 13633536 | tf_op jit(solution)/shard_map/dot_general | solution.py:32
  80.6 1.2 fusion.25
  83.2 10.8 %fusion.14 = bf16[64,8,8,128]{3,2,1,0:T(8,128)(2,1)} fusion(bf16[512,4096]{1,0:T(8,128)(2,1)} %all-gather.4.cloned.1.call-done, bf16[4096,1024]{1,0:T(8,128)(2,1)} %param.11, f32[512]{0:T(512)S(1)} %multiply_exponential_fusion), kind=kOutput, calls=%fused_computation.23 | convolution fusion | flops 4298113024 | bytes 13633536 | tf_op jit(solution)/shard_map/dot_general | solution.py:32
  94.0 61.2 %all-gather.6.cloned.1.call-done = f32[256,128,128]{2,1,0:T(8,128)} async-done(((f32[8,128,128]{2,1,0:T(8,128)}), f32[256,128,128]{2,1,0:T(8,128)}) %all-gather.6.cloned.1.call-update) | async-done | bytes 16777232 | tf_op jit(solution)/shard_map/all_gather | solution.py:12
  155.1 40.0 %while.14 = (s32[]{:T(128)}, f32[8,128,128]{2,1,0:T(8,128)S(1)}, s32[]{:T(128)}, f32[32,8,128,128]{3,2,1,0:T(8,128)}, s32[]{:T(128)}, /*index=5*/s32[]{:T(128)}) while((s32[]{:T(128)}, f32[8,128,128]{2,1,0:T(8,128)S(1)}, s32[]{:T(128)}, f32[32,8,128,128]{3,2,1,0:T(8,128)}, s32[]{:T(128)}, /*index=5*/s32[]{:T(128)}) %tuple.42), condition=%wide.region_1.2_spmd.clone, body=%wide.region_0.1_spmd.clone.sunk | while | flops 393220 | bytes 1572965 | solution.py:20
  156.4 1.2 add_select_fusion.2
  157.6 1.2 add_select_fusion.2
  158.9 1.2 add_select_fusion.2
  160.1 1.2 add_select_fusion.2
  161.4 1.2 add_select_fusion.2
  162.6 1.2 add_select_fusion.2
  163.9 1.2 add_select_fusion.2
  165.2 1.2 add_select_fusion.2
  166.4 1.2 add_select_fusion.2
  167.7 1.2 add_select_fusion.2
  180.2 1.2 add_select_fusion.2
  190.2 1.2 add_select_fusion.2
  195.2 3.1 %fusion.17 = f32[8,128,512]{2,1,0:T(8,128)} fusion(bf16[64,8,8,128]{3,2,1,0:T(8,128)(2,1)} %fusion.14, f32[8,128,128]{2,1,0:T(8,128)S(1)} %get-tuple-element.84, f32[8,128,128]{2,1,0:T(8,128)S(1)} %copy-done), kind=kOutput, calls=%fused_computation.25 | convolution fusion | flops 134610944 | bytes 4194304 | tf_op jit(solution)/shard_map/bshd,bhde->bshe/dot_general | solution.py:52
  198.2 6.1 %fusion.10 = (f32[512,8]{0,1:T(8,128)S(1)}, f32[8,128,512]{2,1,0:T(8,128)}) fusion(f32[8,128,512]{2,1,0:T(8,128)} %fusion.17, bf16[512,8,128]{0,2,1:T(8,128)(2,1)S(1)} %bitcast.45, f32[512,512]{1,0:T(8,128)} %fusion.19, bf16[512,8,128]{0,2,1:T(8,128)(2,1)S(1)} %bitcast.43, bf16[64,8,8,128]{3,2,1,0:T(8,128)(2,1)} %fusion.14), kind=kOutput, calls=%fused_computation.18 | convolution fusion | flops 1079504896 | bytes 8404992 | tf_op jit(solution)/shard_map/bhst,bthe->bshe/dot_general | solution.py:56
  204.4 1.9 fusion.12
  206.3 9.5 %convolution_convert_fusion = bf16[512,4096]{1,0:T(8,128)(2,1)} fusion(bf16[512,1024]{0,1:T(8,128)(2,1)S(1)} %bitcast.46, bf16[1024,4096]{1,0:T(8,128)(2,1)} %param.15), kind=kOutput, calls=%fused_computation.6 | convolution fusion | flops 4297064448 | bytes 13631488 | tf_op jit(solution)/shard_map/dot_general | solution.py:66
  215.8 46.3 %reduce-scatter.2.cloned.1.call-done = bf16[128,4096]{1,0:T(8,128)(2,1)} async-done(((bf16[512,4096]{1,0:T(8,128)(2,1)}), bf16[128,4096]{1,0:T(8,128)(2,1)}) %reduce-scatter.2.cloned.1.call-update) | async-done | bytes 1048592 | tf_op jit(solution)/shard_map/reduce_scatter | solution.py:65
  (36 shorter events, 28.4 us)
Async XLA Ops:
  6.5 53.9 %all-gather.4.cloned.1.call-start = ((), (), s32[]{:S(2)}) async-start(), calls=%async_computation.1 | async-start | bytes 5242880 | tf_op jit(solution)/shard_map/all_gather | solution.py:30
  7.3 147.9 %all-gather.6.cloned.1.call-start = ((), (), s32[]{:S(2)}) async-start(), calls=%async_computation.3 | async-start | bytes 17301504 | tf_op jit(solution)/shard_map/all_gather | solution.py:12
  81.8 180.2 %reduce-scatter.2.cloned.1.call-start = ((), (), s32[]{:S(2)}) async-start(), calls=%async_computation.2 | async-start | bytes 5242880 | tf_op jit(solution)/shard_map/reduce_scatter | solution.py:65
  94.0 101.2 %copy-start = (f32[8,128,128]{2,1,0:T(8,128)S(1)}, f32[8,128,128]{2,1,0:T(8,128)}, u32[]{:S(2)}) copy-start(f32[8,128,128]{2,1,0:T(8,128)} %fusion.25) | copy-start | bytes 1572868
  198.2 6.1 %copy-start.1 = (f32[1024]{0:T(1024)S(1)}, f32[1024]{0:T(1024)}, u32[]{:S(2)}) copy-start(f32[1024]{0:T(1024)} %param.14) | copy-start | bytes 12292
Sparse Core Ops, SparseCore 0:
  9.0 51.4 all-gather.3
  82.0 73.1 all-gather.5
  215.9 46.0 reduce-scatter.1
where the time goes:
time: 270 us; the launch traced here: 269 us
  waiting for transfers between devices  161 us (60%)
  matrix products  49.7 us (18%)
  other arithmetic  42.9 us (16%)
  between operations  13.2 us (5%)
    all_gather x1, waiting for transfers between devices, prefix(): everything = lax.all_gather(x, axis)  61.2 us
    all_gather x1, waiting for transfers between devices, on_device(): piece = lax.all_gather(codes, 'tp', axis=1, tiled=True)  52.5 us
    reduce_scatter x1, waiting for transfers between devices, on_device(): lax.psum_scatter(jnp.dot(normed, w_out, preferred_element_type=jnp.float3...  46.3 us
    select_n x32, other arithmetic, step(): return jnp.where(reached, new, before)  39.3 us
    dot_general x3, matrix products, on_device(): jnp.dot(piece, weight, preferred_element_type=jnp.float32)  29.8 us
    dot_general x1, matrix products, on_device(): jnp.dot(normed, w_out, preferred_element_type=jnp.float32)  9.5 us
    dot_general x1, matrix products, on_device(): jnp.einsum('bhst,bthe->bshe', scores, value_b, preferred_element_type=jnp...  6.13 us
  transfers between devices with their start and end apart: 3, of which 3 were waited for; matrix products, arithmetic and copies ran while one was open for 5% of the time, Pallas kernels for 0%

commit v1 on v0

v1 whole, which is shorter than its diff:
```python
import functools

import jax
import jax.numpy as jnp
from jax import lax
from jax.experimental import pallas as pl
from jax.experimental.pallas import tpu as pltpu
from jax.sharding import PartitionSpec as P

HD = 128
BLK = 512
TN = 256
MIB = 1 << 20


f32 = jnp.float32
bf16 = jnp.bfloat16
HBM = pl.BlockSpec(memory_space=pltpu.HBM)
VM = pl.BlockSpec(memory_space=pltpu.VMEM)


def ring(n, d):
    return [(i, (i + d) % n) for i in range(n)]


def chip(y, x, c):
    return (y * 4 + x) * 2 + c


def exchange(move, first):
    found = []
    for y in range(4):
        for x in range(4):
            for c in range(2):
                along_y = (c == 0) == first
                to = (move(y), x, c) if along_y else (y, move(x), c)
                found.append((chip(y, x, c), chip(*to)))
    return found


SWAP = [(s, s ^ 1) for s in range(32)]


def near(v):
    return v ^ 1


def mirror(v):
    return 3 - v


def shift(v, pairs, axis="tp"):
    return lax.ppermute(v, axis, pairs)


def in_hbm(*arrays):
    return [pltpu.with_memory_space_constraint(v, pltpu.HBM) for v in arrays]


def dot(a, b):
    return jnp.dot(a, b, preferred_element_type=f32)


def params(limit, **more):
    return pltpu.CompilerParams(vmem_limit_bytes=limit * MIB, **more)


def cost(flops, nbytes):
    return pl.CostEstimate(flops=flops, bytes_accessed=nbytes, transcendentals=0)


OWN, LEFT, RIGHT, FAR, CORE0, ODD_A, HIGH_A, ODD_B, HIGH_B = range(9)
SCALARS = pl.BlockSpec(memory_space=pltpu.SMEM)


def project_kernel(count, have, info, *refs):
    xs, refs = refs[:count], refs[count:]
    ws, refs = refs[: 3 * count], refs[3 * count :]
    accs, outs = (refs[:3], refs[3:]) if have else (None, refs)
    cols = pl.ds(pl.multiple_of(pl.program_id(0) * TN, TN), TN)
    for i in range(3):
        total = accs[i][:, cols] if have else None
        for j in range(count):
            term = dot(xs[j][...], ws[3 * j + i][...])
            total = term if total is None else total + term
        outs[i][:, cols] = total


def project(info, pieces, blocks, weights, accs):
    count, have = len(pieces), accs is not None
    tok, depth = pieces[0].shape
    width = weights[0].shape[1]

    def wspec(j):
        device, half = blocks[j]
        return pl.BlockSpec((depth, TN), lambda n, i: (2 * i[device] + half, n))

    return pl.pallas_call(
        functools.partial(project_kernel, count, have),
        out_shape=[pltpu.VMEM((tok, width), f32)] * 3,
        grid_spec=pltpu.PrefetchScalarGridSpec(
            num_scalar_prefetch=1,
            grid=(width // TN,),
            in_specs=[VM] * count
            + [wspec(j) for j in range(count) for _ in range(3)]
            + ([VM] * 3 if have else []),
            out_specs=[VM] * 3,
        ),
        compiler_params=params(16),
        cost_estimate=cost(6 * count * tok * depth * width, 6 * count * depth * width),
    )(info, *pieces, *(list(weights) * count), *(accs or ()))


def fetch_kernel(rows, info, wq, wk, wv, wo, fq, fk, fv, fo, sem):
    start = pl.multiple_of(info[FAR] * rows, rows)
    copies = [
        pltpu.make_async_copy(w.at[pl.ds(start, rows), :], f, sem.at[n])
        for n, (w, f) in enumerate(((wk, fk), (wv, fv), (wq, fq)))
    ]
    copies.append(pltpu.make_async_copy(wo, fo, sem.at[3]))
    for c in copies:
        c.start()
    for c in copies:
        c.wait()


def fetch(info, rows, weights, w_out):
    width = weights[0].shape[1]
    return pl.pallas_call(
        functools.partial(fetch_kernel, rows),
        out_shape=[pltpu.VMEM((rows, width), bf16)] * 3 + [pltpu.VMEM(w_out.shape, bf16)],
        in_specs=[SCALARS] + [HBM] * 4,
        out_specs=[VM] * 4,
        scratch_shapes=[pltpu.SemaphoreType.DMA((4,))],
        compiler_params=params(8),
        cost_estimate=cost(0, 14 * MIB),
    )(info, *weights, w_out)


def feature(t):
    return jnp.where(t > 0, t + 1.0, jnp.exp(t)).astype(bf16)


def last_kv_kernel(info, xa, xb, wk, wv, acck, accv, scale, fk, vb, mine, other, state):
    half = xa.shape[1]

    @pl.loop(0, fk.shape[1] // TN)
    def _(n):
        cols = pl.ds(pl.multiple_of(n * TN, TN), TN)

        def full(w, acc):
            t = acc[:, cols] + dot(xa[...], w[pl.ds(0, half), cols])
            return (t + dot(xb[...], w[pl.ds(half, half), cols])) * scale[...]

        k = feature(full(wk, acck))
        v = full(wv, accv).astype(bf16)
        fk[:, cols] = k
        vb[:, cols] = v
        for h in range(TN // HD):
            part = slice(h * HD, (h + 1) * HD)
            state[n * (TN // HD) + h] = lax.dot_general(
                k[:, part], v[:, part], (((0,), (0,)), ((), ())), preferred_element_type=f32
            )

    count = mine.shape[0]
    for h in range(count):
        mine[h] = state[(1 - info[CORE0]) * count + h]
        other[h] = state[info[CORE0] * count + h].astype(bf16)


def last_kv(info, xa, xb, wk, wv, acck, accv, scale):
    tok, width = acck.shape
    return pl.pallas_call(
        last_kv_kernel,
        out_shape=[
            pltpu.VMEM((tok, width), bf16),
            pltpu.VMEM((tok, width), bf16),
            pltpu.VMEM((width // HD // 2, HD, HD), f32),
            pltpu.VMEM((width // HD // 2, HD, HD), bf16),
        ],
        in_specs=[SCALARS] + [VM] * 7,
        out_specs=[VM] * 4,
        scratch_shapes=[pltpu.VMEM((width // HD, HD, HD), f32)],
        compiler_params=params(12),
        cost_estimate=cost(4 * tok * 1024 * width, 8 * MIB),
    )(info, xa, xb, wk, wv, acck, accv, scale)


def last_q_kernel(xa, xb, w, acc, scale, fq):
    half = xa.shape[1]

    @pl.loop(0, fq.shape[1] // TN)
    def _(n):
        cols = pl.ds(pl.multiple_of(n * TN, TN), TN)
        t = acc[:, cols] + dot(xa[...], w[pl.ds(0, half), cols])
        fq[:, cols] = feature((t + dot(xb[...], w[pl.ds(half, half), cols])) * scale[...])


def last_q(xa, xb, w, acc, scale):
    tok, width = acc.shape
    return pl.pallas_call(
        last_q_kernel,
        out_shape=pltpu.VMEM((tok, width), bf16),
        in_specs=[VM] * 5,
        out_specs=VM,
        compiler_params=params(12),
        cost_estimate=cost(2 * tok * 1024 * width, 4 * MIB),
    )(xa, xb, w, acc, scale)


def within_kernel(first, fq, fk, vb, out):
    rows = BLK // 2
    row = lax.broadcasted_iota(jnp.int32, (rows, rows), 0)
    col = lax.broadcasted_iota(jnp.int32, (rows, rows), 1)
    keep = row >= col

    @pl.loop(0, out.shape[1] // HD)
    def _(h):
        cols = pl.ds(pl.multiple_of((first + h) * HD, HD), HD)
        ocols = pl.ds(pl.multiple_of(h * HD, HD), HD)

        def scores(q, k):
            return lax.dot_general(
                q, k, (((1,), (1,)), ((), ())), preferred_element_type=f32
            )

        for i in range(2):
            mine = pl.ds(i * rows, rows)
            q = fq[mine, cols]
            s = jnp.where(keep, scores(q, fk[mine, cols]), 0.0).astype(bf16)
            y = dot(s, vb[mine, cols])
            if i == 1:
                early = pl.ds(0, rows)
                s = scores(q, fk[early, cols]).astype(bf16)
                y = y + dot(s, vb[early, cols])
            out[mine, ocols] = y


def within(first, heads, fq, fk, vb):
    tok = fq.shape[0]
    return pl.pallas_call(
        functools.partial(within_kernel, first),
        out_shape=pltpu.VMEM((tok, heads * HD), f32),
        in_specs=[VM] * 3,
        out_specs=VM,
        compiler_params=params(12),
        cost_estimate=cost(4 * heads * tok * tok * HD, 4 * MIB),
    )(fq, fk, vb)


def share_kernel(place, sides, heads, info, fq, ylow, yhigh, own, back, gain, wo, *refs):
    outs, o = refs[:-1], refs[-1]
    rows = o.shape[0]
    mine = pl.ds(pl.multiple_of(info[place] * rows, rows), rows)
    for h in range(heads):
        cols = slice(h * HD, (h + 1) * HD)
        near_y = ylow if h < heads // 2 else yhigh
        g = h % (heads // 2)
        took = own if h < heads // 2 else back
        gave = back if h < heads // 2 else own
        state = jnp.where(info[CORE0] == 1, took[g], gave[g])
        y = near_y[mine, g * HD : (g + 1) * HD] + dot(fq[mine, cols], state)
        ms = jnp.mean(y * y, axis=-1, keepdims=True)
        o[:, cols] = (y * lax.rsqrt(ms + 1e-05) * gain[:, cols]).astype(bf16)
    half = wo.shape[1] // 2
    for side, out in zip(sides, outs):

        @pl.loop(0, half // 512)
        def _(n):
            src = pl.ds(pl.multiple_of(side * half + n * 512, 512), 512)
            dst = pl.ds(pl.multiple_of(n * 512, 512), 512)
            out[:, dst] = dot(o[...], wo[:, src]).astype(out.dtype)


def share(info, place, sides, types, fq, ylow, yhigh, own, back, gain, wo):
    tok, width = fq.shape
    rows, half = tok // 4, wo.shape[1] // 2
    return pl.pallas_call(
        functools.partial(share_kernel, place, sides, width // HD),
        out_shape=[pltpu.VMEM((rows, half), t) for t in types],
        in_specs=[SCALARS] + [VM] * 7,
        out_specs=[VM] * len(sides),
        scratch_shapes=[pltpu.VMEM((rows, width), bf16)],
        compiler_params=params(12),
        cost_estimate=cost(2 * rows * width * half * len(sides), 4 * MIB),
    )(info, fq, ylow, yhigh, own, back, gain, wo)


def small(body, outs, info, *ins):
    def kernel(info, *refs):
        flag = [info[n].astype(f32) for n in range(info.shape[0])]
        for h in range(refs[0].shape[0]):
            got = [r[h].astype(f32) for r in refs[: len(ins)]]
            for ref, value in zip(refs[len(ins) :], body(flag, *got)):
                ref[h] = value.astype(ref.dtype)

    count = ins[0].shape[0]
    return pl.pallas_call(
        kernel,
        out_shape=[pltpu.VMEM((count, HD, HD), t) for t in outs],
        in_specs=[SCALARS] + [VM] * len(ins),
        out_specs=[VM] * len(outs),
        compiler_params=params(4),
        cost_estimate=cost(1000, MIB // 2),
    )(info, *ins)


def before_this(info, mine, other):
    def send(v, pairs):
        return shift(v, pairs, "seq")

    theirs = send(other, SWAP)
    (both,) = small(lambda i, m, t: (m + t,), (bf16,), info, mine, theirs)
    r1 = send(both, exchange(near, True))
    (two,) = small(lambda i, m, t, r1: (m + t + r1,), (bf16,), info, mine, theirs, r1)
    r2 = send(two, exchange(mirror, True))

    def third(i, m, t, r1, r2):
        earlier = i[ODD_A] * r1 + i[HIGH_A] * r2
        four = m + t + r1 + r2
        first = i[CORE0] * earlier + (1.0 - i[CORE0]) * four
        return earlier, first, first

    earlier, first, sent = small(third, (f32, f32, bf16), info, mine, theirs, r1, r2)
    r3 = send(sent, exchange(near, False))
    t3 = send(both, exchange(near, False))

    def fourth(i, earlier, first, r3, t3, m, t):
        v = first + r3 + i[CORE0] * (1.0 - i[HIGH_B]) * (m + t + t3)
        seen = i[CORE0] + (1.0 - i[CORE0]) * i[ODD_B]
        return v, earlier + seen * r3 + i[CORE0] * i[ODD_B] * t3

    v, earlier = small(fourth, (bf16, f32), info, earlier, first, r3, t3, mine, theirs)
    r4 = send(v, exchange(mirror, False))

    def fifth(i, earlier, r4, m, t):
        before = earlier + (i[CORE0] + (1.0 - i[CORE0]) * i[HIGH_B]) * r4
        return before + (1.0 - i[CORE0]) * t, before + i[CORE0] * m

    own, partner = small(fifth, (bf16, bf16), info, earlier, r4, mine, theirs)
    return own, send(partner, SWAP)


def on_device(codes, exponents, w_query, w_key, w_value, norm_gain, w_out):
    z = lax.axis_index("tp")
    s = lax.axis_index("seq")
    core, x, y = s % 2, (s // 2) % 4, s // 8
    first, second = jnp.where(core == 0, y, x), jnp.where(core == 0, x, y)
    info = jnp.stack(
        [
            z,
            (z + 3) % 4,
            (z + 1) % 4,
            (z + 2) % 4,
            1 - core,
            first % 2,
            first // 2,
            second % 2,
            second // 2,
        ]
    ).astype(jnp.int32)
    _, part = codes.shape
    hp = part // 2
    width = w_query.shape[1]
    heads = width // HD
    scale = jnp.exp2(exponents.astype(f32))[:, None]
    gain = norm_gain.reshape(1, width)
    codes, info, scale, gain = lax.optimization_barrier((codes, info, scale, gain))
    up, down = ring(4, 1), ring(4, -1)
    weights, w_out = in_hbm(w_query, w_key, w_value), in_hbm(w_out)[0]

    a, b = codes[:, :hp], codes[:, hp:]
    a_left = shift(a, up)
    b_right = shift(b, down)
    b_left = shift(b, up)
    a_right = shift(a, down)
    a_far = shift(a_left, up)
    b_far = shift(b_right, down)

    accs = project(info, (a, b), ((OWN, 0), (OWN, 1)), weights, None)
    wq_far, wk_far, wv_far, wo = fetch(info, part, weights, w_out)
    accs = project(info, (a_left, b_right), ((LEFT, 0), (RIGHT, 1)), weights, accs)
    accs = project(info, (b_left, a_right), ((LEFT, 1), (RIGHT, 0)), weights, accs)
    feat_k, value_b, mine, other = last_kv(
        info, a_far, b_far, wk_far, wv_far, accs[1], accs[2], scale
    )
    own, back = before_this(info, mine, other)
    feat_q = last_q(a_far, b_far, wq_far, accs[0], scale)
    ylow = within(0, heads // 2, feat_q, feat_k, value_b)
    yhigh = within(heads // 2, heads // 2, feat_q, feat_k, value_b)

    rest = (feat_q, ylow, yhigh, own, back, gain, wo)
    (u_far,) = share(info, FAR, (0,), (bf16,), *rest)
    u_pass = shift(u_far, up)
    (l_far,) = share(info, FAR, (1,), (bf16,), *rest)
    l_pass = shift(l_far, down)
    l_next, u_next = share(info, RIGHT, (1, 0), (bf16, f32), *rest)
    l_low = shift(l_next, up)
    u_prev, l_prev = share(info, LEFT, (0, 1), (bf16, f32), *rest)
    u_high = shift(u_prev, down)
    u, l = share(info, OWN, (0, 1), (f32, f32), *rest)
    u_low = shift((u_next + u_pass.astype(f32)).astype(bf16), up)
    l_high = shift((l_prev + l_pass.astype(f32)).astype(bf16), down)
    u = u + u_high.astype(f32) + u_low.astype(f32)
    l = l + l_low.astype(f32) + l_high.astype(f32)
    return jnp.concatenate([u, l], 1).astype(bf16)


def solution(mesh):
    in_specs = (
        P("seq", "tp"),
        P("seq"),
        P(None, "tp"),
        P(None, "tp"),
        P(None, "tp"),
        P("tp"),
        P("tp", None),
    )
    out_specs = P(("seq", "tp"), None)

    return jax.shard_map(
        on_device, mesh=mesh, in_specs=in_specs, out_specs=out_specs, check_vma=False
    )
```

time: 270 us -> 126 us (0.47)
  waiting for transfers between devices: 161 us -> 36.8 us
  Pallas kernels: 0 us -> 54.4 us
  matrix products: 49.7 us -> 0 us
  other arithmetic: 42.9 us -> 2.42 us
  starting transfers between devices: 0.26 us -> 30.6 us
  between operations: 13.2 us -> 0.25 us
    all_gather x2 -> x0, waiting for transfers between devices: 114 us -> none  [the longest x1 61.2 us: prefix(): everything = lax.all_gather(x, axis)]
    pallas_call x0 -> x18, Pallas kernels: none -> 54.4 us  [the longest x3 19.4 us: project(): pl.pallas_call(functools.partial(project_kernel, count, have), out_shape=...]
    dot_general x7 -> x0, matrix products: 49.7 us -> none  [the longest x3 29.8 us: on_device(): jnp.dot(piece, weight, preferred_element_type=jnp.float32)]
    reduce_scatter x1 -> x0, waiting for transfers between devices: 46.3 us -> none  [on_device(): lax.psum_scatter(jnp.dot(normed, w_out, preferred_element_type=jnp.float3...]
    select_n x33 -> x0, other arithmetic: 40.3 us -> none  [the longest x32 39.3 us: step(): return jnp.where(reached, new, before)]
    ppermute x0 -> x19, waiting for transfers between devices: none -> 36.8 us  [shift(): return lax.ppermute(v, axis, pairs)]
    ppermute x0 -> x19, starting transfers between devices: none -> 30.6 us  [shift(): return lax.ppermute(v, axis, pairs)]
  transfers between devices with their start and end apart: 3 -> 19, of which waited for: 3 -> 12; matrix products, arithmetic and copies ran while one was open for 5% -> 0% of each run, Pallas kernels for 0% -> 36%
where the time goes in v1:
time: 126 us
  Pallas kernels  54.4 us (43%)
  waiting for transfers between devices  36.8 us (29%)
  starting transfers between devices  30.6 us (24%)
  other arithmetic  2.42 us (2%)
  local copies, waits for them, and re-layouts  1.51 us (1%)
    ppermute x19, waiting for transfers between devices, shift(): return lax.ppermute(v, axis, pairs)  36.8 us
    ppermute x19, starting transfers between devices, shift(): return lax.ppermute(v, axis, pairs)  30.6 us
    pallas_call x3, Pallas kernels, project(): pl.pallas_call(functools.partial(project_kernel, count, have), out_shape=...  19.4 us
    pallas_call x5, Pallas kernels, share(): pl.pallas_call(functools.partial(share_kernel, place, sides, width // HD)...  15 us
    pallas_call x1, Pallas kernels, fetch(): pl.pallas_call(functools.partial(fetch_kernel, rows), out_shape=[pltpu.VM...  5.84 us
    pallas_call x1, Pallas kernels, last_kv(): pl.pallas_call(last_kv_kernel, out_shape=[pltpu.VMEM((tok, width), bf16),...  4.75 us
    pallas_call x2, Pallas kernels, within(): pl.pallas_call(functools.partial(within_kernel, first), out_shape=pltpu.V...  4.41 us
    pallas_call x5, Pallas kernels, small(): pl.pallas_call(kernel, out_shape=[pltpu.VMEM((count, HD, HD), t) for t in...  3.08 us
  transfers between devices with their start and end apart: 19, of which 12 were waited for; matrix products, arithmetic and copies ran while one was open for 0% of the time, Pallas kernels for 36%

profile of v1, /device:TPU:1, one launch (start us, length us, event | category | flops | bytes accessed | tf_op | source)
XLA Modules:
  0.0 125.9 jit_solution(12260431274130605115)
XLA Ops:
  2.1 4.6 %collective-permute-start.2 = (bf16[512,512]{1,0:T(8,128)(2,1)S(1)}, bf16[512,512]{1,0:T(8,128)(2,1)S(1)}, u32[]{:S(2)}, u32[]{:S(2)}) collective-permute-start(bf16[512,512]{1,0:T(8,128)(2,1)S(1)} %get-tuple-element.73.refs_1_), channel_id=1, source_target_pairs={{0,3},{1,0},{2,1},{3,2},{4,7},{5,4},{6,5},{7,6},{8,11},{9,8},{10,9... | collective-permute-start | bytes 1572872 | tf_op jit(solution)/shard_map/ppermute | solution.py:53
  6.7 2.7 %collective-permute-start.5 = (bf16[512,512]{1,0:T(8,128)(2,1)S(1)}, bf16[512,512]{1,0:T(8,128)(2,1)S(1)}, u32[]{:S(2)}, u32[]{:S(2)}) collective-permute-start(bf16[512,512]{1,0:T(8,128)(2,1)S(1)} %get-tuple-element.74.refs_0_), channel_id=1, source_target_pairs={{0,3},{1,0},{2,1},{3,2},{4,7},{5,4},{6,5},{7,6},{8,11},{9,8},{10,9... | collective-permute-start | bytes 1572872 | tf_op jit(solution)/shard_map/ppermute | solution.py:53
  9.5 5.8 %shard_map.73 = (bf16[1024,1024]{1,0:T(8,128)(2,1)S(1)}, bf16[1024,1024]{1,0:T(8,128)(2,1)S(1)}, bf16[1024,1024]{1,0:T(8,128)(2,1)S(1)}, bf16[1024,4096]{1,0:T(8,128)(2,1)S(1)}) custom-call(s32[9]{0:T(128)S(1)} %stack.39.info, bf16[4096,1024]{1,0:T(8,128)(2,1)} %refs_5_.5, bf16[4096,1024]{1,0:T(8,128)(2,1)} %refs_6_.5, bf16[4096,1024]{1,0:T(8,128)(2,1)} %refs_7_.5, ...), custom_call_target="tpu_custom_call" | custom-call | bytes 14680064 | tf_op jit(solution)/shard_map/pallas_call | solution.py:129
  15.4 6.5 %shard_map.74 = (f32[512,1024]{1,0:T(8,128)S(1)}, f32[512,1024]{1,0:T(8,128)S(1)}, f32[512,1024]{1,0:T(8,128)S(1)}) custom-call(s32[9]{0:T(128)S(1)} %stack.39.info, bf16[512,512]{1,0:T(8,128)(2,1)S(1)} %get-tuple-element.74.refs_0_, bf16[512,512]{1,0:T(8,128)(2,1)S(1)} %get-tuple-element.73.refs_1_, bf16[4096,1024]{1,0:T(8,128)(2,1)} %refs_5_.5, ...), custom_call_target="tpu_custom_call" | custom-call | flops 3221225472 | bytes 6291456 | tf_op jit(solution)/shard_map/pallas_call | solution.py:98
  23.4 6.5 %shard_map.75 = (f32[512,1024]{1,0:T(8,128)S(1)}, f32[512,1024]{1,0:T(8,128)S(1)}, f32[512,1024]{1,0:T(8,128)S(1)}) custom-call(s32[9]{0:T(128)S(1)} %stack.39.info, bf16[512,512]{1,0:T(8,128)(2,1)S(1)} %collective-permute-done.refs_0_, bf16[512,512]{1,0:T(8,128)(2,1)S(1)} %collective-permute-done.2.refs_1_, bf16[4096,1024]{1,0:T(8,128)(2,1)} %refs_5_.5, ...), custom_call_target="tpu_custom_call" | custom-call | flops 3221225472 | bytes 6291456 | tf_op jit(solution)/shard_map/pallas_call | solution.py:98
  31.7 6.5 %shard_map.76 = (f32[512,1024]{1,0:T(8,128)S(1)}, f32[512,1024]{1,0:T(8,128)S(1)}, f32[512,1024]{1,0:T(8,128)S(1)}) custom-call(s32[9]{0:T(128)S(1)} %stack.39.info, bf16[512,512]{1,0:T(8,128)(2,1)S(1)} %collective-permute-done.4.refs_0_, bf16[512,512]{1,0:T(8,128)(2,1)S(1)} %collective-permute-done.5.refs_1_, bf16[4096,1024]{1,0:T(8,128)(2,1)} %refs_5_.5, ...), custom_call_target="tpu_custom_call" | custom-call | flops 3221225472 | bytes 6291456 | tf_op jit(solution)/shard_map/pallas_call | solution.py:98
  39.8 3.1 %collective-permute-done.1.xa = bf16[512,512]{1,0:T(8,128)(2,1)S(1)} collective-permute-done((bf16[512,512]{1,0:T(8,128)(2,1)S(1)}, bf16[512,512]{1,0:T(8,128)(2,1)S(1)}, u32[]{:S(2)}, u32[]{:S(2)}) %collective-permute-start.1) | collective-permute-done | bytes 524320 | tf_op jit(solution)/shard_map/ppermute | solution.py:53
  42.9 4.8 %shard_map.78 = (bf16[512,1024]{1,0:T(8,128)(2,1)S(1)}, bf16[512,1024]{1,0:T(8,128)(2,1)S(1)}, f32[4,128,128]{2,1,0:T(8,128)S(1)}, bf16[4,128,128]{2,1,0:T(8,128)(2,1)S(1)}) custom-call(s32[9]{0:T(128)S(1)} %stack.39.info, bf16[512,512]{1,0:T(8,128)(2,1)S(1)} %collective-permute-done.1.xa, bf16[512,512]{1,0:T(8,128)(2,1)S(1)} %collective-permute-done.3.xb, ...), custom_call_target="tpu_custom_call" | custom-call | flops 2147483648 | bytes 8388608 | tf_op jit(solution)/shard_map/pallas_call | solution.py:173
  52.4 2.9 %collective-permute-done.7.refs_2_ = bf16[4,128,128]{2,1,0:T(8,128)(2,1)S(1)} collective-permute-done((bf16[4,128,128]{2,1,0:T(8,128)(2,1)S(1)}, bf16[4,128,128]{2,1,0:T(8,128)(2,1)S(1)}, u32[]{:S(2)}, u32[]{:S(2)}) %collective-permute-start.7) | collective-permute-done | bytes 131104 | tf_op jit(solution)/shard_map/ppermute | solution.py:53
  55.9 2.6 %collective-permute-start.8 = (bf16[4,128,128]{2,1,0:T(8,128)(2,1)S(1)}, bf16[4,128,128]{2,1,0:T(8,128)(2,1)S(1)}, u32[]{:S(2)}, u32[]{:S(2)}) collective-permute-start(bf16[4,128,128]{2,1,0:T(8,128)(2,1)S(1)} %shard_map.82), channel_id=1, source_target_pairs={{0,96},{4,28},{8,104},{12,20},{16,112},{20,12},{24,120},{28,4},{32... | collective-permute-start | bytes 393224 | tf_op jit(solution)/shard_map/ppermute | solution.py:53
  63.1 2.5 %collective-permute-done.9.refs_2_ = bf16[4,128,128]{2,1,0:T(8,128)(2,1)S(1)} collective-permute-done((bf16[4,128,128]{2,1,0:T(8,128)(2,1)S(1)}, bf16[4,128,128]{2,1,0:T(8,128)(2,1)S(1)}, u32[]{:S(2)}, u32[]{:S(2)}) %collective-permute-start.9) | collective-permute-done | bytes 131104 | tf_op jit(solution)/shard_map/ppermute | solution.py:53
  66.2 2.8 %collective-permute-start.11 = (bf16[4,128,128]{2,1,0:T(8,128)(2,1)S(1)}, bf16[4,128,128]{2,1,0:T(8,128)(2,1)S(1)}, u32[]{:S(2)}, u32[]{:S(2)}) collective-permute-start(bf16[4,128,128]{2,1,0:T(8,128)(2,1)S(1)} %get-tuple-element.62), channel_id=1, source_target_pairs={{0,24},{4,100},{8,16},{12,108},{16,8},{20,116},{24,0},{28,124},{32... | collective-permute-start | bytes 393224 | tf_op jit(solution)/shard_map/ppermute | solution.py:53
  69.1 2.4 %collective-permute-done.11.refs_1_ = bf16[4,128,128]{2,1,0:T(8,128)(2,1)S(1)} collective-permute-done((bf16[4,128,128]{2,1,0:T(8,128)(2,1)S(1)}, bf16[4,128,128]{2,1,0:T(8,128)(2,1)S(1)}, u32[]{:S(2)}, u32[]{:S(2)}) %collective-permute-start.11) | collective-permute-done | bytes 131104 | tf_op jit(solution)/shard_map/ppermute | solution.py:53
  72.0 4.7 %collective-permute-start.12 = (bf16[4,128,128]{2,1,0:T(8,128)(2,1)S(1)}, bf16[4,128,128]{2,1,0:T(8,128)(2,1)S(1)}, u32[]{:S(2)}, u32[]{:S(2)}) collective-permute-start(bf16[4,128,128]{2,1,0:T(8,128)(2,1)S(1)} %get-tuple-element.64), channel_id=1, source_target_pairs={{0,4},{4,0},{8,12},{12,8},{16,20},{20,16},{24,28},{28,24},{32,36},... | collective-permute-start | bytes 393224 | tf_op jit(solution)/shard_map/ppermute | solution.py:53
  78.6 2.2 %shard_map.80.yhigh = f32[512,512]{1,0:T(8,128)S(1)} custom-call(bf16[512,1024]{1,0:T(8,128)(2,1)S(1)} %shard_map.77.fq, bf16[512,1024]{1,0:T(8,128)(2,1)S(1)} %get-tuple-element.54.fk, bf16[512,1024]{1,0:T(8,128)(2,1)S(1)} %get-tuple-element.55.vb), custom_call_target="tpu_custom_call" | custom-call | flops 536870912 | bytes 4194304 | tf_op jit(solution)/shard_map/pallas_call | solution.py:241
  83.1 2.2 %shard_map.90 = bf16[128,2048]{1,0:T(8,128)(2,1)S(1)} custom-call(s32[9]{0:T(128)S(1)} %stack.39.info, bf16[512,1024]{1,0:T(8,128)(2,1)S(1)} %shard_map.77.fq, f32[512,512]{1,0:T(8,128)S(1)} %shard_map.79.ylow, f32[512,512]{1,0:T(8,128)S(1)} %shard_map.80.yhigh, bf16[4,128,128]{2,1,0:T(8,128)(2,1)S(1)} %get-tuple-element.63.own, ...), custom_call_target="tpu_custom_call" | custom-call | flops 536870912 | bytes 4194304 | tf_op jit(solution)/shard_map/pallas_call | solution.py:278
  85.4 2.2 %shard_map.89 = bf16[128,2048]{1,0:T(8,128)(2,1)S(1)} custom-call(s32[9]{0:T(128)S(1)} %stack.39.info, bf16[512,1024]{1,0:T(8,128)(2,1)S(1)} %shard_map.77.fq, f32[512,512]{1,0:T(8,128)S(1)} %shard_map.79.ylow, f32[512,512]{1,0:T(8,128)S(1)} %shard_map.80.yhigh, bf16[4,128,128]{2,1,0:T(8,128)(2,1)S(1)} %get-tuple-element.63.own, ...), custom_call_target="tpu_custom_call" | custom-call | flops 536870912 | bytes 4194304 | tf_op jit(solution)/shard_map/pallas_call | solution.py:278
  89.1 3.5 %shard_map.88 = (bf16[128,2048]{1,0:T(8,128)(2,1)S(1)}, f32[128,2048]{1,0:T(8,128)S(1)}) custom-call(s32[9]{0:T(128)S(1)} %stack.39.info, bf16[512,1024]{1,0:T(8,128)(2,1)S(1)} %shard_map.77.fq, f32[512,512]{1,0:T(8,128)S(1)} %shard_map.79.ylow, f32[512,512]{1,0:T(8,128)S(1)} %shard_map.80.yhigh, bf16[4,128,128]{2,1,0:T(8,128)(2,1)S(1)} %get-tuple-element.63.own, ...), custom_call_target="tpu_custom_call" | custom-call | flops 1073741824 | bytes 4194304 | tf_op jit(solution)/shard_map/pallas_call | solution.py:278
  92.9 3.5 %shard_map.87 = (bf16[128,2048]{1,0:T(8,128)(2,1)S(1)}, f32[128,2048]{1,0:T(8,128)S(1)}) custom-call(s32[9]{0:T(128)S(1)} %stack.39.info, bf16[512,1024]{1,0:T(8,128)(2,1)S(1)} %shard_map.77.fq, f32[512,512]{1,0:T(8,128)S(1)} %shard_map.79.ylow, f32[512,512]{1,0:T(8,128)S(1)} %shard_map.80.yhigh, bf16[4,128,128]{2,1,0:T(8,128)(2,1)S(1)} %get-tuple-element.63.own, ...), custom_call_target="tpu_custom_call" | custom-call | flops 1073741824 | bytes 4194304 | tf_op jit(solution)/shard_map/pallas_call | solution.py:278
  96.4 2.7 %collective-permute-start.13 = (bf16[128,2048]{1,0:T(8,128)(2,1)S(1)}, bf16[128,2048]{1,0:T(8,128)(2,1)S(1)}, u32[]{:S(2)}, u32[]{:S(2)}) collective-permute-start(bf16[128,2048]{1,0:T(8,128)(2,1)S(1)} %get-tuple-element.68), channel_id=1, source_target_pairs={{0,3},{1,0},{2,1},{3,2},{4,7},{5,4},{6,5},{7,6},{8,11},{9,8},{10,9... | collective-permute-start | bytes 1572872 | tf_op jit(solution)/shard_map/ppermute | solution.py:53
  102.5 3.5 %shard_map.86 = (f32[128,2048]{1,0:T(8,128)S(1)}, f32[128,2048]{1,0:T(8,128)S(1)}) custom-call(s32[9]{0:T(128)S(1)} %stack.39.info, bf16[512,1024]{1,0:T(8,128)(2,1)S(1)} %shard_map.77.fq, f32[512,512]{1,0:T(8,128)S(1)} %shard_map.79.ylow, f32[512,512]{1,0:T(8,128)S(1)} %shard_map.80.yhigh, bf16[4,128,128]{2,1,0:T(8,128)(2,1)S(1)} %get-tuple-element.63.own, ...), custom_call_target="tpu_custom_call" | custom-call | flops 1073741824 | bytes 4194304 | tf_op jit(solution)/shard_map/pallas_call | solution.py:278
  106.0 7.3 %collective-permute-done.16 = bf16[128,2048]{1,0:T(8,128)(2,1)S(1)} collective-permute-done((bf16[128,2048]{1,0:T(8,128)(2,1)S(1)}, bf16[128,2048]{1,0:T(8,128)(2,1)S(1)}, u32[]{:S(2)}, u32[]{:S(2)}) %collective-permute-start.16) | collective-permute-done | bytes 524320 | tf_op jit(solution)/shard_map/ppermute | solution.py:53
  113.4 7.5 %collective-permute-done.18 = bf16[128,2048]{1,0:T(8,128)(2,1)S(1)} collective-permute-done((bf16[128,2048]{1,0:T(8,128)(2,1)S(1)}, bf16[128,2048]{1,0:T(8,128)(2,1)S(1)}, u32[]{:S(2)}, u32[]{:S(2)}) %collective-permute-start.18) | collective-permute-done | bytes 524320 | tf_op jit(solution)/shard_map/ppermute | solution.py:53
  121.1 3.5 %collective-permute-done.15 = bf16[128,2048]{1,0:T(8,128)(2,1)S(1)} collective-permute-done((bf16[128,2048]{1,0:T(8,128)(2,1)S(1)}, bf16[128,2048]{1,0:T(8,128)(2,1)S(1)}, u32[]{:S(2)}, u32[]{:S(2)}) %collective-permute-start.15) | collective-permute-done | bytes 524320 | tf_op jit(solution)/shard_map/ppermute | solution.py:53
  (43 shorter events, 29.1 us)
Async XLA Ops:
  2.1 19.8 %collective-permute-start.2 = (bf16[512,512]{1,0:T(8,128)(2,1)S(1)}, bf16[512,512]{1,0:T(8,128)(2,1)S(1)}, u32[]{:S(2)}, u32[]{:S(2)}) collective-permute-start(bf16[512,512]{1,0:T(8,128)(2,1)S(1)} %get-tuple-element.73.refs_1_), channel_id=1, source_target_pairs={{0,3},{1,0},{2,1},{3,2},{4,7},{5,4},{6,5},{7,6},{8,11},{9,8},{10,9... | collective-permute-start | bytes 1572872 | tf_op jit(solution)/shard_map/ppermute | solution.py:53
  6.7 16.7 %collective-permute-start = (bf16[512,512]{1,0:T(8,128)(2,1)S(1)}, bf16[512,512]{1,0:T(8,128)(2,1)S(1)}, u32[]{:S(2)}, u32[]{:S(2)}) collective-permute-start(bf16[512,512]{1,0:T(8,128)(2,1)S(1)} %get-tuple-element.74.refs_0_), channel_id=1, source_target_pairs={{0,1},{1,2},{2,3},{3,0},{4,5},{5,6},{6,7},{7,4},{8,9},{9,10},{10,1... | collective-permute-start | bytes 1572872 | tf_op jit(solution)/shard_map/ppermute | solution.py:53
  6.7 25.0 %collective-permute-start.4 = (bf16[512,512]{1,0:T(8,128)(2,1)S(1)}, bf16[512,512]{1,0:T(8,128)(2,1)S(1)}, u32[]{:S(2)}, u32[]{:S(2)}) collective-permute-start(bf16[512,512]{1,0:T(8,128)(2,1)S(1)} %get-tuple-element.73.refs_1_), channel_id=1, source_target_pairs={{0,1},{1,2},{2,3},{3,0},{4,5},{5,6},{6,7},{7,4},{8,9},{9,10},{10,1... | collective-permute-start | bytes 1572872 | tf_op jit(solution)/shard_map/ppermute | solution.py:53
  6.7 25.0 %collective-permute-start.5 = (bf16[512,512]{1,0:T(8,128)(2,1)S(1)}, bf16[512,512]{1,0:T(8,128)(2,1)S(1)}, u32[]{:S(2)}, u32[]{:S(2)}) collective-permute-start(bf16[512,512]{1,0:T(8,128)(2,1)S(1)} %get-tuple-element.74.refs_0_), channel_id=1, source_target_pairs={{0,3},{1,0},{2,1},{3,2},{4,7},{5,4},{6,5},{7,6},{8,11},{9,8},{10,9... | collective-permute-start | bytes 1572872 | tf_op jit(solution)/shard_map/ppermute | solution.py:53
  21.9 17.9 %collective-permute-start.3 = (bf16[512,512]{1,0:T(8,128)(2,1)S(1)}, bf16[512,512]{1,0:T(8,128)(2,1)S(1)}, u32[]{:S(2)}, u32[]{:S(2)}) collective-permute-start(bf16[512,512]{1,0:T(8,128)(2,1)S(1)} %collective-permute-done.2.refs_1_), channel_id=1, source_target_pairs={{0,3},{1,0},{2,1},{3,2},{4,7},{5,4},{6,5},{7,6},{8,11},{9,8},{10,9... | collective-permute-start | bytes 1572872 | tf_op jit(solution)/shard_map/ppermute | solution.py:53
  23.4 19.5 %collective-permute-start.1 = (bf16[512,512]{1,0:T(8,128)(2,1)S(1)}, bf16[512,512]{1,0:T(8,128)(2,1)S(1)}, u32[]{:S(2)}, u32[]{:S(2)}) collective-permute-start(bf16[512,512]{1,0:T(8,128)(2,1)S(1)} %collective-permute-done.refs_0_), channel_id=1, source_target_pairs={{0,1},{1,2},{2,3},{3,0},{4,5},{5,6},{6,7},{7,4},{8,9},{9,10},{10,1... | collective-permute-start | bytes 1572872 | tf_op jit(solution)/shard_map/ppermute | solution.py:53
  47.7 2.9 %collective-permute-start.6 = (bf16[4,128,128]{2,1,0:T(8,128)(2,1)S(1)}, bf16[4,128,128]{2,1,0:T(8,128)(2,1)S(1)}, u32[]{:S(2)}, u32[]{:S(2)}) collective-permute-start(bf16[4,128,128]{2,1,0:T(8,128)(2,1)S(1)} %get-tuple-element.57), channel_id=1, source_target_pairs={{0,4},{4,0},{8,12},{12,8},{16,20},{20,16},{24,28},{28,24},{32,36},... | collective-permute-start | bytes 393224 | tf_op jit(solution)/shard_map/ppermute | solution.py:53
  51.1 4.2 %collective-permute-start.7 = (bf16[4,128,128]{2,1,0:T(8,128)(2,1)S(1)}, bf16[4,128,128]{2,1,0:T(8,128)(2,1)S(1)}, u32[]{:S(2)}, u32[]{:S(2)}) collective-permute-start(bf16[4,128,128]{2,1,0:T(8,128)(2,1)S(1)} %shard_map.81), channel_id=1, source_target_pairs={{0,32},{4,12},{8,40},{12,4},{16,48},{20,28},{24,56},{28,20},{32,0}... | collective-permute-start | bytes 393224 | tf_op jit(solution)/shard_map/ppermute | solution.py:53
  55.9 5.1 %collective-permute-start.8 = (bf16[4,128,128]{2,1,0:T(8,128)(2,1)S(1)}, bf16[4,128,128]{2,1,0:T(8,128)(2,1)S(1)}, u32[]{:S(2)}, u32[]{:S(2)}) collective-permute-start(bf16[4,128,128]{2,1,0:T(8,128)(2,1)S(1)} %shard_map.82), channel_id=1, source_target_pairs={{0,96},{4,28},{8,104},{12,20},{16,112},{20,12},{24,120},{28,4},{32... | collective-permute-start | bytes 393224 | tf_op jit(solution)/shard_map/ppermute | solution.py:53
  58.5 4.6 %collective-permute-start.10 = (bf16[4,128,128]{2,1,0:T(8,128)(2,1)S(1)}, bf16[4,128,128]{2,1,0:T(8,128)(2,1)S(1)}, u32[]{:S(2)}, u32[]{:S(2)}) collective-permute-start(bf16[4,128,128]{2,1,0:T(8,128)(2,1)S(1)} %shard_map.81), channel_id=1, source_target_pairs={{0,8},{4,36},{8,0},{12,44},{16,24},{20,52},{24,16},{28,60},{32,40}... | collective-permute-start | bytes 393224 | tf_op jit(solution)/shard_map/ppermute | solution.py:53
  61.7 3.9 %collective-permute-start.9 = (bf16[4,128,128]{2,1,0:T(8,128)(2,1)S(1)}, bf16[4,128,128]{2,1,0:T(8,128)(2,1)S(1)}, u32[]{:S(2)}, u32[]{:S(2)}) collective-permute-start(bf16[4,128,128]{2,1,0:T(8,128)(2,1)S(1)} %get-tuple-element.60), channel_id=1, source_target_pairs={{0,8},{4,36},{8,0},{12,44},{16,24},{20,52},{24,16},{28,60},{32,40}... | collective-permute-start | bytes 393224 | tf_op jit(solution)/shard_map/ppermute | solution.py:53
  66.2 5.2 %collective-permute-start.11 = (bf16[4,128,128]{2,1,0:T(8,128)(2,1)S(1)}, bf16[4,128,128]{2,1,0:T(8,128)(2,1)S(1)}, u32[]{:S(2)}, u32[]{:S(2)}) collective-permute-start(bf16[4,128,128]{2,1,0:T(8,128)(2,1)S(1)} %get-tuple-element.62), channel_id=1, source_target_pairs={{0,24},{4,100},{8,16},{12,108},{16,8},{20,116},{24,0},{28,124},{32... | collective-permute-start | bytes 393224 | tf_op jit(solution)/shard_map/ppermute | solution.py:53
  72.0 11.0 %collective-permute-start.12 = (bf16[4,128,128]{2,1,0:T(8,128)(2,1)S(1)}, bf16[4,128,128]{2,1,0:T(8,128)(2,1)S(1)}, u32[]{:S(2)}, u32[]{:S(2)}) collective-permute-start(bf16[4,128,128]{2,1,0:T(8,128)(2,1)S(1)} %get-tuple-element.64), channel_id=1, source_target_pairs={{0,4},{4,0},{8,12},{12,8},{16,20},{20,16},{24,28},{28,24},{32,36},... | collective-permute-start | bytes 393224 | tf_op jit(solution)/shard_map/ppermute | solution.py:53
  80.8 2.2 %copy-start = (f32[1024]{0:T(1024)S(1)}, f32[1024]{0:T(1024)}, u32[]{:S(2)}) copy-start(f32[1024]{0:T(1024)} %param.12) | copy-start | bytes 12292
  85.3 13.8 %collective-permute-start.17 = (bf16[128,2048]{1,0:T(8,128)(2,1)S(1)}, bf16[128,2048]{1,0:T(8,128)(2,1)S(1)}, u32[]{:S(2)}, u32[]{:S(2)}) collective-permute-start(bf16[128,2048]{1,0:T(8,128)(2,1)S(1)} %shard_map.90), channel_id=1, source_target_pairs={{0,3},{1,0},{2,1},{3,2},{4,7},{5,4},{6,5},{7,6},{8,11},{9,8},{10,9... | collective-permute-start | bytes 1572872 | tf_op jit(solution)/shard_map/ppermute | solution.py:53
  87.6 14.5 %collective-permute-start.14 = (bf16[128,2048]{1,0:T(8,128)(2,1)S(1)}, bf16[128,2048]{1,0:T(8,128)(2,1)S(1)}, u32[]{:S(2)}, u32[]{:S(2)}) collective-permute-start(bf16[128,2048]{1,0:T(8,128)(2,1)S(1)} %shard_map.89), channel_id=1, source_target_pairs={{0,1},{1,2},{2,3},{3,0},{4,5},{5,6},{6,7},{7,4},{8,9},{9,10},{10,1... | collective-permute-start | bytes 1572872 | tf_op jit(solution)/shard_map/ppermute | solution.py:53
  92.6 20.7 %collective-permute-start.16 = (bf16[128,2048]{1,0:T(8,128)(2,1)S(1)}, bf16[128,2048]{1,0:T(8,128)(2,1)S(1)}, u32[]{:S(2)}, u32[]{:S(2)}) collective-permute-start(bf16[128,2048]{1,0:T(8,128)(2,1)S(1)} %get-tuple-element.71), channel_id=1, source_target_pairs={{0,1},{1,2},{2,3},{3,0},{4,5},{5,6},{6,7},{7,4},{8,9},{9,10},{10,1... | collective-permute-start | bytes 1572872 | tf_op jit(solution)/shard_map/ppermute | solution.py:53
  96.4 24.7 %collective-permute-start.13 = (bf16[128,2048]{1,0:T(8,128)(2,1)S(1)}, bf16[128,2048]{1,0:T(8,128)(2,1)S(1)}, u32[]{:S(2)}, u32[]{:S(2)}) collective-permute-start(bf16[128,2048]{1,0:T(8,128)(2,1)S(1)} %get-tuple-element.68), channel_id=1, source_target_pairs={{0,3},{1,0},{2,1},{3,2},{4,7},{5,4},{6,5},{7,6},{8,11},{9,8},{10,9... | collective-permute-start | bytes 1572872 | tf_op jit(solution)/shard_map/ppermute | solution.py:53
  99.3 21.6 %collective-permute-start.18 = (bf16[128,2048]{1,0:T(8,128)(2,1)S(1)}, bf16[128,2048]{1,0:T(8,128)(2,1)S(1)}, u32[]{:S(2)}, u32[]{:S(2)}) collective-permute-start(bf16[128,2048]{1,0:T(8,128)(2,1)S(1)} %add_convert_fusion.1), channel_id=1, source_target_pairs={{0,3},{1,0},{2,1},{3,2},{4,7},{5,4},{6,5},{7,6},{8,11},{9,8},{10,9... | collective-permute-start | bytes 1572872 | tf_op jit(solution)/shard_map/ppermute | solution.py:53
  102.3 22.3 %collective-permute-start.15 = (bf16[128,2048]{1,0:T(8,128)(2,1)S(1)}, bf16[128,2048]{1,0:T(8,128)(2,1)S(1)}, u32[]{:S(2)}, u32[]{:S(2)}) collective-permute-start(bf16[128,2048]{1,0:T(8,128)(2,1)S(1)} %add_convert_fusion.3), channel_id=1, source_target_pairs={{0,1},{1,2},{2,3},{3,0},{4,5},{5,6},{6,7},{7,4},{8,9},{9,10},{10,1... | collective-permute-start | bytes 1572872 | tf_op jit(solution)/shard_map/ppermute | solution.py:53

commit v2 on v1

v2 whole, which is shorter than its diff:
```python
import functools

import jax
import jax.numpy as jnp
from jax import lax
from jax.experimental import pallas as pl
from jax.experimental.pallas import tpu as pltpu
from jax.sharding import PartitionSpec as P

HD = 128
BLK = 512
TN = 256
MIB = 1 << 20


f32 = jnp.float32
bf16 = jnp.bfloat16
HBM = pl.BlockSpec(memory_space=pltpu.HBM)
VM = pl.BlockSpec(memory_space=pltpu.VMEM)


def ring(n, d):
    return [(i, (i + d) % n) for i in range(n)]


def chip(y, x, c):
    return (y * 4 + x) * 2 + c


def exchange(move, first):
    found = []
    for y in range(4):
        for x in range(4):
            for c in range(2):
                along_y = (c == 0) == first
                to = (move(y), x, c) if along_y else (y, move(x), c)
                found.append((chip(y, x, c), chip(*to)))
    return found


SWAP = [(s, s ^ 1) for s in range(32)]


def near(v):
    return v ^ 1


def mirror(v):
    return 3 - v


def shift(v, pairs, axis="tp"):
    return lax.ppermute(v, axis, pairs)


def in_hbm(*arrays):
    return [pltpu.with_memory_space_constraint(v, pltpu.HBM) for v in arrays]


def dot(a, b):
    return jnp.dot(a, b, preferred_element_type=f32)


def params(limit, **more):
    return pltpu.CompilerParams(vmem_limit_bytes=limit * MIB, **more)


def cost(flops, nbytes):
    return pl.CostEstimate(flops=flops, bytes_accessed=nbytes, transcendentals=0)


OWN, LEFT, RIGHT, FAR, CORE0 = range(5)
SCALARS = pl.BlockSpec(memory_space=pltpu.SMEM)


def project_kernel(count, have, info, *refs):
    xs, refs = refs[:count], refs[count:]
    ws, refs = refs[: 3 * count], refs[3 * count :]
    accs, outs = (refs[:3], refs[3:]) if have else (None, refs)
    cols = pl.ds(pl.multiple_of(pl.program_id(0) * TN, TN), TN)
    for i in range(3):
        total = accs[i][:, cols] if have else None
        for j in range(count):
            term = dot(xs[j][...], ws[3 * j + i][...])
            total = term if total is None else total + term
        outs[i][:, cols] = total


def project(info, pieces, blocks, weights, accs):
    count, have = len(pieces), accs is not None
    tok, depth = pieces[0].shape
    width = weights[0].shape[1]

    def wspec(j):
        device, half = blocks[j]
        return pl.BlockSpec((depth, TN), lambda n, i: (2 * i[device] + half, n))

    return pl.pallas_call(
        functools.partial(project_kernel, count, have),
        out_shape=[pltpu.VMEM((tok, width), f32)] * 3,
        grid_spec=pltpu.PrefetchScalarGridSpec(
            num_scalar_prefetch=1,
            grid=(width // TN,),
            in_specs=[VM] * count
            + [wspec(j) for j in range(count) for _ in range(3)]
            + ([VM] * 3 if have else []),
            out_specs=[VM] * 3,
        ),
        compiler_params=params(16),
        cost_estimate=cost(6 * count * tok * depth * width, 6 * count * depth * width),
    )(info, *pieces, *(list(weights) * count), *(accs or ()))


def split_kernel(codes, a, b, sem):
    half = a.shape[1]
    copies = [
        pltpu.make_async_copy(codes.at[:, pl.ds(0, half)], a, sem.at[0]),
        pltpu.make_async_copy(codes.at[:, pl.ds(half, half)], b, sem.at[1]),
    ]
    for c in copies:
        c.start()
    for c in copies:
        c.wait()


def split(codes):
    tok, part = codes.shape
    return pl.pallas_call(
        split_kernel,
        out_shape=[pltpu.VMEM((tok, part // 2), bf16)] * 2,
        in_specs=[HBM],
        out_specs=[VM] * 2,
        scratch_shapes=[pltpu.SemaphoreType.DMA((2,))],
        compiler_params=params(4),
        cost_estimate=cost(0, 2 * MIB),
    )(codes)


def fetch_kernel(rows, info, wq, wk, wv, wo, fq, fk, fv, fo, sem):
    start = pl.multiple_of(info[FAR] * rows, rows)
    copies = [
        pltpu.make_async_copy(w.at[pl.ds(start, rows), :], f, sem.at[n])
        for n, (w, f) in enumerate(((wk, fk), (wv, fv), (wq, fq)))
    ]
    copies.append(pltpu.make_async_copy(wo, fo, sem.at[3]))
    for c in copies:
        c.start()
    for c in copies:
        c.wait()


def fetch(info, rows, weights, w_out):
    width = weights[0].shape[1]
    return pl.pallas_call(
        functools.partial(fetch_kernel, rows),
        out_shape=[pltpu.VMEM((rows, width), bf16)] * 3 + [pltpu.VMEM(w_out.shape, bf16)],
        in_specs=[SCALARS] + [HBM] * 4,
        out_specs=[VM] * 4,
        scratch_shapes=[pltpu.SemaphoreType.DMA((4,))],
        compiler_params=params(8),
        cost_estimate=cost(0, 14 * MIB),
    )(info, *weights, w_out)


def feature(t):
    return jnp.where(t > 0, t + 1.0, jnp.exp(t)).astype(bf16)


def last_kv_kernel(part, info, xa, xb, wk, wv, acck, accv, scale, fk, vb, state):
    half, width = xa.shape[1], fk.shape[1]
    core = 1 - info[CORE0]
    start = (core if part == 0 else 1 - core) * width

    for n in range(width // TN):
        cols = pl.ds(pl.multiple_of(start + n * TN, TN), TN)
        ocols = slice(n * TN, (n + 1) * TN)

        def full(w, acc):
            t = acc[:, cols] + dot(xa[...], w[pl.ds(0, half), cols])
            return (t + dot(xb[...], w[pl.ds(half, half), cols])) * scale[...]

        k = feature(full(wk, acck))
        v = full(wv, accv).astype(bf16)
        fk[:, ocols] = k
        vb[:, ocols] = v
        for h in range(TN // HD):
            cut = slice(h * HD, (h + 1) * HD)
            state[n * (TN // HD) + h] = lax.dot_general(
                k[:, cut], v[:, cut], (((0,), (0,)), ((), ())), preferred_element_type=f32
            ).astype(state.dtype)


def last_kv(part, info, xa, xb, wk, wv, acck, accv, scale):
    tok, width = acck.shape[0], acck.shape[1] // 2
    return pl.pallas_call(
        functools.partial(last_kv_kernel, part),
        out_shape=[
            pltpu.VMEM((tok, width), bf16),
            pltpu.VMEM((tok, width), bf16),
            pltpu.VMEM((width // HD, HD, HD), f32 if part == 0 else bf16),
        ],
        in_specs=[SCALARS] + [VM] * 7,
        out_specs=[VM] * 3,
        compiler_params=params(12),
        cost_estimate=cost(4 * tok * 1024 * width, 4 * MIB),
    )(info, xa, xb, wk, wv, acck, accv, scale)


def last_q_kernel(xa, xb, w, acc, scale, fq):
    half = xa.shape[1]

    @pl.loop(0, fq.shape[1] // TN)
    def _(n):
        cols = pl.ds(pl.multiple_of(n * TN, TN), TN)
        t = acc[:, cols] + dot(xa[...], w[pl.ds(0, half), cols])
        fq[:, cols] = feature((t + dot(xb[...], w[pl.ds(half, half), cols])) * scale[...])


def last_q(xa, xb, w, acc, scale):
    tok, width = acc.shape
    return pl.pallas_call(
        last_q_kernel,
        out_shape=pltpu.VMEM((tok, width), bf16),
        in_specs=[VM] * 5,
        out_specs=VM,
        compiler_params=params(12),
        cost_estimate=cost(2 * tok * 1024 * width, 4 * MIB),
    )(xa, xb, w, acc, scale)


def within_kernel(part, info, fq, fk, vb, out):
    rows, width = BLK // 2, out.shape[1]
    row = lax.broadcasted_iota(jnp.int32, (rows, rows), 0)
    col = lax.broadcasted_iota(jnp.int32, (rows, rows), 1)
    keep = row >= col
    core = 1 - info[CORE0]
    start = (core if part == 0 else 1 - core) * width

    @pl.loop(0, width // HD)
    def _(h):
        qcols = pl.ds(pl.multiple_of(start + h * HD, HD), HD)
        cols = pl.ds(pl.multiple_of(h * HD, HD), HD)

        def scores(q, k):
            return lax.dot_general(
                q, k, (((1,), (1,)), ((), ())), preferred_element_type=f32
            )

        for i in range(2):
            mine = pl.ds(i * rows, rows)
            q = fq[mine, qcols]
            s = jnp.where(keep, scores(q, fk[mine, cols]), 0.0).astype(bf16)
            y = dot(s, vb[mine, cols])
            if i == 1:
                early = pl.ds(0, rows)
                s = scores(q, fk[early, cols]).astype(bf16)
                y = y + dot(s, vb[early, cols])
            out[mine, cols] = y


def within(part, info, fq, fk, vb):
    tok, width = fk.shape
    return pl.pallas_call(
        functools.partial(within_kernel, part),
        out_shape=pltpu.VMEM((tok, width), f32),
        in_specs=[SCALARS] + [VM] * 3,
        out_specs=VM,
        compiler_params=params(12),
        cost_estimate=cost(4 * width * tok * tok, 4 * MIB),
    )(info, fq, fk, vb)


def normed(info, place, fq, ys, states, gain, o):
    rows, width = o.shape
    mine = pl.ds(pl.multiple_of(info[place] * rows, rows), rows)
    core = 1 - info[CORE0]
    for part in range(2):
        start = (core if part == 0 else 1 - core) * (width // 2)
        for g in range(width // HD // 2):
            cols = pl.ds(pl.multiple_of(start + g * HD, HD), HD)
            y = ys[part][mine, g * HD : (g + 1) * HD] + dot(fq[mine, cols], states[part][g])
            ms = jnp.mean(y * y, axis=-1, keepdims=True)
            o[:, cols] = (y * lax.rsqrt(ms + 1e-05) * gain[:, cols]).astype(bf16)


def project_out(o, wo, spans, outs):
    for (start, size), out in zip(spans, outs):

        @pl.loop(0, size // 512)
        def _(n):
            src = pl.ds(pl.multiple_of(start + n * 512, 512), 512)
            dst = pl.ds(pl.multiple_of(n * 512, 512), 512)
            out[:, dst] = dot(o[...], wo[:, src]).astype(out.dtype)


def first_kernel(place, spans, info, fq, y0, y1, own, back, gain, wo, o, *outs):
    normed(info, place, fq, (y0, y1), (own, back), gain, o)
    project_out(o, wo, spans, outs)


def first_share(info, place, spans, types, fq, y0, y1, own, back, gain, wo):
    tok, width = fq.shape
    rows = tok // 4
    return pl.pallas_call(
        functools.partial(first_kernel, place, spans),
        out_shape=[pltpu.VMEM((rows, width), bf16)]
        + [pltpu.VMEM((rows, size), t) for (_, size), t in zip(spans, types)],
        in_specs=[SCALARS] + [VM] * 7,
        out_specs=[VM] * (1 + len(spans)),
        compiler_params=params(12),
        cost_estimate=cost(2 * rows * width * sum(n for _, n in spans), 4 * MIB),
    )(info, fq, y0, y1, own, back, gain, wo)


def more_kernel(spans, o, wo, *outs):
    project_out(o, wo, spans, outs)


def more_share(spans, types, o, wo):
    rows, width = o.shape
    return pl.pallas_call(
        functools.partial(more_kernel, spans),
        out_shape=[pltpu.VMEM((rows, size), t) for (_, size), t in zip(spans, types)],
        in_specs=[VM] * 2,
        out_specs=[VM] * len(spans),
        compiler_params=params(12),
        cost_estimate=cost(2 * rows * width * sum(n for _, n in spans), 4 * MIB),
    )(o, wo)


def finish_kernel(side, own, one, two, *refs):
    out, total, sem = refs[-3:]
    half = own.shape[1]
    sums = own[...] + one[...].astype(f32) + two[...].astype(f32)
    total[...] = sums.astype(bf16)
    copy = pltpu.make_async_copy(total, out.at[:, pl.ds(side * half, half)], sem)
    copy.start()
    copy.wait()


def finish(side, own, one, two, out):
    rows, half = own.shape
    given = () if out is None else (out,)
    return pl.pallas_call(
        functools.partial(finish_kernel, side),
        out_shape=pltpu.HBM((rows, 2 * half), bf16),
        in_specs=[VM] * 3 + [HBM] * len(given),
        out_specs=HBM,
        input_output_aliases={3: 0} if given else {},
        scratch_shapes=[pltpu.VMEM((rows, half), bf16), pltpu.SemaphoreType.DMA],
        compiler_params=params(8),
        cost_estimate=cost(rows * half, 3 * MIB),
    )(own, one, two, *given)


def before_this(flags, mine, other):
    core0, core1, odd_a, high_a, first_low, early_t, early_p, all_p = flags

    def send(v, pairs):
        return shift(v.astype(bf16), pairs, "seq").astype(f32)

    theirs = send(other, SWAP)
    both = mine + theirs
    r1 = send(both, exchange(near, True))
    two = both + r1
    r2 = send(two, exchange(mirror, True))
    t3 = send(both, exchange(near, False))
    earlier = odd_a * r1 + high_a * r2
    first = core0 * earlier + core1 * (two + r2)
    r3 = send(first, exchange(near, False))
    v = first + r3 + first_low * (both + t3)
    r4 = send(v, exchange(mirror, False))
    prefix = earlier + early_p * r3 + early_t * t3 + all_p * r4
    own = (prefix + core1 * theirs).astype(bf16)
    return own, send(prefix + core0 * mine, SWAP).astype(bf16)


def on_device(codes, exponents, w_query, w_key, w_value, norm_gain, w_out):
    z = lax.axis_index("tp")
    s = lax.axis_index("seq")
    core, x, y = s % 2, (s // 2) % 4, s // 8
    first, second = jnp.where(core == 0, y, x), jnp.where(core == 0, x, y)
    info = jnp.stack([z, (z + 3) % 4, (z + 1) % 4, (z + 2) % 4, 1 - core]).astype(jnp.int32)
    core0, core1 = core == 0, core == 1
    flags = [
        v.astype(f32)
        for v in (
            core0,
            core1,
            first % 2,
            first // 2,
            core0 & (second < 2),
            core0 & (second % 2 == 1),
            core0 | (second % 2 == 1),
            core0 | (second >= 2),
        )
    ]
    _, part = codes.shape
    width = w_query.shape[1]
    half = w_out.shape[1] // 2
    scale = jnp.exp2(exponents.astype(f32))[:, None]
    gain = norm_gain.reshape(1, width)
    codes, info, *flags = lax.optimization_barrier((codes, info, *flags))
    up, down = ring(4, 1), ring(4, -1)
    weights, w_out = in_hbm(w_query, w_key, w_value), in_hbm(w_out)[0]

    a, b = split(in_hbm(codes)[0])
    a_left = shift(a, up)
    b_right = shift(b, down)
    b_left = shift(b, up)
    a_right = shift(a, down)
    a_far = shift(a_left, up)
    b_far = shift(b_right, down)

    accs = project(info, (a, b), ((OWN, 0), (OWN, 1)), weights, None)
    wq_far, wk_far, wv_far, wo = fetch(info, part, weights, w_out)
    accs = project(info, (a_left, b_right), ((LEFT, 0), (RIGHT, 1)), weights, accs)
    accs = project(info, (b_left, a_right), ((LEFT, 1), (RIGHT, 0)), weights, accs)
    last = (a_far, b_far, wk_far, wv_far, accs[1], accs[2], scale)
    k1, v1, other = last_kv(1, info, *last)
    k0, v0, mine = last_kv(0, info, *last)
    own, back = before_this(flags, mine, other)
    feat_q = last_q(a_far, b_far, wq_far, accs[0], scale)
    y0 = within(0, info, feat_q, k0, v0)
    y1 = within(1, info, feat_q, k1, v1)

    rest = (feat_q, y0, y1, own, back, gain, wo)
    o, u_far = first_share(info, FAR, ((0, half),), (bf16,), *rest)
    u_pass = shift(u_far, up)
    (l_far,) = more_share(((half, half),), (bf16,), o, wo)
    l_pass = shift(l_far, down)
    _, l_next, u_next = first_share(
        info, RIGHT, ((half, half), (0, half)), (bf16, f32), *rest
    )
    l_low = shift(l_next, up)
    _, u_prev, l_prev = first_share(info, LEFT, ((0, half), (half, half)), (bf16, f32), *rest)
    u_high = shift(u_prev, down)
    _, u, l = first_share(info, OWN, ((0, half), (half, half)), (f32, f32), *rest)
    u_low = shift((u_next + u_pass.astype(f32)).astype(bf16), up)
    l_high = shift((l_prev + l_pass.astype(f32)).astype(bf16), down)
    out = finish(0, u, u_high, u_low, None)
    return finish(1, l, l_low, l_high, out)


def solution(mesh):
    in_specs = (
        P("seq", "tp"),
        P("seq"),
        P(None, "tp"),
        P(None, "tp"),
        P(None, "tp"),
        P("tp"),
        P("tp", None),
    )
    out_specs = P(("seq", "tp"), None)

    return jax.shard_map(
        on_device, mesh=mesh, in_specs=in_specs, out_specs=out_specs, check_vma=False
    )
```

time: 126 us -> 124 us (0.984)
  waiting for transfers between devices: 36.8 us -> 31.7 us
  starting transfers between devices: 30.6 us -> 33.8 us
  Pallas kernels: 54.4 us -> 55.9 us
  local copies, waits for them, and re-layouts: 1.51 us -> 0.24 us
    ppermute x19, waiting for transfers between devices: 36.8 us -> 31.7 us  [shift(): return lax.ppermute(v, axis, pairs)]
    ppermute x19, starting transfers between devices: 30.6 us -> 33.8 us  [shift(): return lax.ppermute(v, axis, pairs)]
    pallas_call x13 -> x12, Pallas kernels: 27.3 us -> 28.8 us  [the longest x4 14 us: first_share(): pl.pallas_call(functools.partial(first_kernel, place, spans), out_shape=[...]
    slice x1 -> x0, local copies, waits for them, and re-layouts: 1.28 us -> none  [on_device(): a, b = (codes[:, :hp], codes[:, hp:])]
  transfers between devices with their start and end apart: 19 -> 19, of which waited for: 12 -> 10; matrix products, arithmetic and copies ran while one was open for 0% -> 1% of each run, Pallas kernels for 36% -> 40%
where the time goes in v2:
time: 124 us
  Pallas kernels  55.9 us (45%)
  starting transfers between devices  33.8 us (27%)
  waiting for transfers between devices  31.7 us (26%)
  other arithmetic  1.51 us (1%)
    ppermute x19, starting transfers between devices, shift(): return lax.ppermute(v, axis, pairs)  33.8 us
    ppermute x19, waiting for transfers between devices, shift(): return lax.ppermute(v, axis, pairs)  31.7 us
    pallas_call x3, Pallas kernels, project(): pl.pallas_call(functools.partial(project_kernel, count, have), out_shape=...  19.4 us
    pallas_call x4, Pallas kernels, first_share(): pl.pallas_call(functools.partial(first_kernel, place, spans), out_shape=[...  14 us
    pallas_call x1, Pallas kernels, fetch(): pl.pallas_call(functools.partial(fetch_kernel, rows), out_shape=[pltpu.VM...  5.84 us
    pallas_call x2, Pallas kernels, within(): pl.pallas_call(functools.partial(within_kernel, part), out_shape=pltpu.VM...  5.49 us
    pallas_call x2, Pallas kernels, last_kv(): pl.pallas_call(functools.partial(last_kv_kernel, part), out_shape=[pltpu....  4.83 us
  transfers between devices with their start and end apart: 19, of which 10 were waited for; matrix products, arithmetic and copies ran while one was open for 1% of the time, Pallas kernels for 40%

profile of v2, /device:TPU:1, one launch (start us, length us, event | category | flops | bytes accessed | tf_op | source)
XLA Modules:
  0.0 123.6 jit_solution(6849769708607916066)
XLA Ops:
  1.3 4.6 %collective-permute-start.5 = (bf16[512,512]{1,0:T(8,128)(2,1)S(1)}, bf16[512,512]{1,0:T(8,128)(2,1)S(1)}, u32[]{:S(2)}, u32[]{:S(2)}) collective-permute-start(bf16[512,512]{1,0:T(8,128)(2,1)S(1)} %get-tuple-element.46.refs_0_), channel_id=1, source_target_pairs={{0,3},{1,0},{2,1},{3,2},{4,7},{5,4},{6,5},{7,6},{8,11},{9,8},{10,9... | collective-permute-start | bytes 1572872 | tf_op jit(solution)/shard_map/ppermute | solution.py:53
  6.0 2.7 %collective-permute-start.2 = (bf16[512,512]{1,0:T(8,128)(2,1)S(1)}, bf16[512,512]{1,0:T(8,128)(2,1)S(1)}, u32[]{:S(2)}, u32[]{:S(2)}) collective-permute-start(bf16[512,512]{1,0:T(8,128)(2,1)S(1)} %get-tuple-element.47.refs_1_), channel_id=1, source_target_pairs={{0,3},{1,0},{2,1},{3,2},{4,7},{5,4},{6,5},{7,6},{8,11},{9,8},{10,9... | collective-permute-start | bytes 1572872 | tf_op jit(solution)/shard_map/ppermute | solution.py:53
  9.5 5.8 %shard_map.74 = (bf16[1024,1024]{1,0:T(8,128)(2,1)S(1)}, bf16[1024,1024]{1,0:T(8,128)(2,1)S(1)}, bf16[1024,1024]{1,0:T(8,128)(2,1)S(1)}, bf16[1024,4096]{1,0:T(8,128)(2,1)S(1)}) custom-call(s32[5]{0:T(128)S(1)} %stack.23.info, bf16[4096,1024]{1,0:T(8,128)(2,1)} %refs_5_.5, bf16[4096,1024]{1,0:T(8,128)(2,1)} %refs_6_.5, bf16[4096,1024]{1,0:T(8,128)(2,1)} %refs_7_.5, ...), custom_call_target="tpu_custom_call" | custom-call | bytes 14680064 | tf_op jit(solution)/shard_map/pallas_call | solution.py:154
  15.3 6.5 %shard_map.75 = (f32[512,1024]{1,0:T(8,128)S(1)}, f32[512,1024]{1,0:T(8,128)S(1)}, f32[512,1024]{1,0:T(8,128)S(1)}) custom-call(s32[5]{0:T(128)S(1)} %stack.23.info, bf16[512,512]{1,0:T(8,128)(2,1)S(1)} %get-tuple-element.46.refs_0_, bf16[512,512]{1,0:T(8,128)(2,1)S(1)} %get-tuple-element.47.refs_1_, bf16[4096,1024]{1,0:T(8,128)(2,1)} %refs_5_.5, ...), custom_call_target="tpu_custom_call" | custom-call | flops 3221225472 | bytes 6291456 | tf_op jit(solution)/shard_map/pallas_call | solution.py:98
  21.9 5.9 %collective-permute-done.2.refs_1_ = bf16[512,512]{1,0:T(8,128)(2,1)S(1)} collective-permute-done((bf16[512,512]{1,0:T(8,128)(2,1)S(1)}, bf16[512,512]{1,0:T(8,128)(2,1)S(1)}, u32[]{:S(2)}, u32[]{:S(2)}) %collective-permute-start.2) | collective-permute-done | bytes 524320 | tf_op jit(solution)/shard_map/ppermute | solution.py:53
  27.8 3.4 %collective-permute-start.3 = (bf16[512,512]{1,0:T(8,128)(2,1)S(1)}, bf16[512,512]{1,0:T(8,128)(2,1)S(1)}, u32[]{:S(2)}, u32[]{:S(2)}) collective-permute-start(bf16[512,512]{1,0:T(8,128)(2,1)S(1)} %collective-permute-done.2.refs_1_), channel_id=1, source_target_pairs={{0,3},{1,0},{2,1},{3,2},{4,7},{5,4},{6,5},{7,6},{8,11},{9,8},{10,9... | collective-permute-start | bytes 1572872 | tf_op jit(solution)/shard_map/ppermute | solution.py:53
  31.2 6.5 %shard_map.76 = (f32[512,1024]{1,0:T(8,128)S(1)}, f32[512,1024]{1,0:T(8,128)S(1)}, f32[512,1024]{1,0:T(8,128)S(1)}) custom-call(s32[5]{0:T(128)S(1)} %stack.23.info, bf16[512,512]{1,0:T(8,128)(2,1)S(1)} %collective-permute-done.refs_0_, bf16[512,512]{1,0:T(8,128)(2,1)S(1)} %collective-permute-done.2.refs_1_, bf16[4096,1024]{1,0:T(8,128)(2,1)} %refs_5_.5, ...), custom_call_target="tpu_custom_call" | custom-call | flops 3221225472 | bytes 6291456 | tf_op jit(solution)/shard_map/pallas_call | solution.py:98
  37.7 6.5 %shard_map.77 = (f32[512,1024]{1,0:T(8,128)S(1)}, f32[512,1024]{1,0:T(8,128)S(1)}, f32[512,1024]{1,0:T(8,128)S(1)}) custom-call(s32[5]{0:T(128)S(1)} %stack.23.info, bf16[512,512]{1,0:T(8,128)(2,1)S(1)} %collective-permute-done.4.refs_0_, bf16[512,512]{1,0:T(8,128)(2,1)S(1)} %collective-permute-done.5.refs_1_, bf16[4096,1024]{1,0:T(8,128)(2,1)} %refs_5_.5, ...), custom_call_target="tpu_custom_call" | custom-call | flops 3221225472 | bytes 6291456 | tf_op jit(solution)/shard_map/pallas_call | solution.py:98
  44.2 2.4 %shard_map.81 = (bf16[512,512]{1,0:T(8,128)(2,1)S(1)}, bf16[512,512]{1,0:T(8,128)(2,1)S(1)}, bf16[4,128,128]{2,1,0:T(8,128)(2,1)S(1)}) custom-call(s32[5]{0:T(128)S(1)} %stack.23.info, bf16[512,512]{1,0:T(8,128)(2,1)S(1)} %collective-permute-done.1.xa, bf16[512,512]{1,0:T(8,128)(2,1)S(1)} %collective-permute-done.3.xb, ...), custom_call_target="tpu_custom_call" | custom-call | flops 1073741824 | bytes 4194304 | tf_op jit(solution)/shard_map/pallas_call | solution.py:195
  48.5 2.4 %shard_map.79 = (bf16[512,512]{1,0:T(8,128)(2,1)S(1)}, bf16[512,512]{1,0:T(8,128)(2,1)S(1)}, f32[4,128,128]{2,1,0:T(8,128)S(1)}) custom-call(s32[5]{0:T(128)S(1)} %stack.23.info, bf16[512,512]{1,0:T(8,128)(2,1)S(1)} %collective-permute-done.1.xa, bf16[512,512]{1,0:T(8,128)(2,1)S(1)} %collective-permute-done.3.xb, ...), custom_call_target="tpu_custom_call" | custom-call | flops 1073741824 | bytes 4194304 | tf_op jit(solution)/shard_map/pallas_call | solution.py:195
  52.3 2.9 %collective-permute-done.7 = bf16[4,128,128]{2,1,0:T(8,128)(2,1)S(1)} collective-permute-done((bf16[4,128,128]{2,1,0:T(8,128)(2,1)S(1)}, bf16[4,128,128]{2,1,0:T(8,128)(2,1)S(1)}, u32[]{:S(2)}, u32[]{:S(2)}) %collective-permute-start.7) | collective-permute-done | bytes 131104 | tf_op jit(solution)/shard_map/ppermute | solution.py:53
  55.2 2.6 %collective-permute-start.8 = (bf16[4,128,128]{2,1,0:T(8,128)(2,1)S(1)}, bf16[4,128,128]{2,1,0:T(8,128)(2,1)S(1)}, u32[]{:S(2)}, u32[]{:S(2)}) collective-permute-start(bf16[4,128,128]{2,1,0:T(8,128)(2,1)S(1)} %fusion.11), channel_id=1, source_target_pairs={{0,96},{4,28},{8,104},{12,20},{16,112},{20,12},{24,120},{28,4},{32... | collective-permute-start | bytes 393224 | tf_op jit(solution)/shard_map/ppermute | solution.py:53
  61.9 2.7 %collective-permute-done.9 = bf16[4,128,128]{2,1,0:T(8,128)(2,1)S(1)} collective-permute-done((bf16[4,128,128]{2,1,0:T(8,128)(2,1)S(1)}, bf16[4,128,128]{2,1,0:T(8,128)(2,1)S(1)}, u32[]{:S(2)}, u32[]{:S(2)}) %collective-permute-start.9) | collective-permute-done | bytes 131104 | tf_op jit(solution)/shard_map/ppermute | solution.py:53
  64.8 2.8 %collective-permute-start.11 = (bf16[4,128,128]{2,1,0:T(8,128)(2,1)S(1)}, bf16[4,128,128]{2,1,0:T(8,128)(2,1)S(1)}, u32[]{:S(2)}, u32[]{:S(2)}) collective-permute-start(bf16[4,128,128]{2,1,0:T(8,128)(2,1)S(1)} %fusion.9), channel_id=1, source_target_pairs={{0,24},{4,100},{8,16},{12,108},{16,8},{20,116},{24,0},{28,124},{32... | collective-permute-start | bytes 393224 | tf_op jit(solution)/shard_map/ppermute | solution.py:53
  70.2 4.0 %collective-permute-start.12 = (bf16[4,128,128]{2,1,0:T(8,128)(2,1)S(1)}, bf16[4,128,128]{2,1,0:T(8,128)(2,1)S(1)}, u32[]{:S(2)}, u32[]{:S(2)}) collective-permute-start(bf16[4,128,128]{2,1,0:T(8,128)(2,1)S(1)} %get-tuple-element.83), channel_id=1, source_target_pairs={{0,4},{4,0},{8,12},{12,8},{16,20},{20,16},{24,28},{28,24},{32,36},... | collective-permute-start | bytes 393224 | tf_op jit(solution)/shard_map/ppermute | solution.py:53
  76.1 2.7 %shard_map.80.y0 = f32[512,512]{1,0:T(8,128)S(1)} custom-call(s32[5]{0:T(128)S(1)} %stack.23.info, bf16[512,1024]{1,0:T(8,128)(2,1)S(1)} %shard_map.78.fq, bf16[512,512]{1,0:T(8,128)(2,1)S(1)} %get-tuple-element.60.fk, bf16[512,512]{1,0:T(8,128)(2,1)S(1)} %get-tuple-element.61.vb), custom_call_target="tpu_custom_call" | custom-call | flops 536870912 | bytes 4194304 | tf_op jit(solution)/shard_map/pallas_call | solution.py:263
  78.9 2.7 %shard_map.82.y1 = f32[512,512]{1,0:T(8,128)S(1)} custom-call(s32[5]{0:T(128)S(1)} %stack.23.info, bf16[512,1024]{1,0:T(8,128)(2,1)S(1)} %shard_map.78.fq, bf16[512,512]{1,0:T(8,128)(2,1)S(1)} %get-tuple-element.62.fk, bf16[512,512]{1,0:T(8,128)(2,1)S(1)} %get-tuple-element.63.vb), custom_call_target="tpu_custom_call" | custom-call | flops 536870912 | bytes 4194304 | tf_op jit(solution)/shard_map/pallas_call | solution.py:263
  85.4 2.7 %collective-permute-start.14 = (bf16[128,2048]{1,0:T(8,128)(2,1)S(1)}, bf16[128,2048]{1,0:T(8,128)(2,1)S(1)}, u32[]{:S(2)}, u32[]{:S(2)}) collective-permute-start(bf16[128,2048]{1,0:T(8,128)(2,1)S(1)} %shard_map.87), channel_id=1, source_target_pairs={{0,3},{1,0},{2,1},{3,2},{4,7},{5,4},{6,5},{7,6},{8,11},{9,8},{10,9... | collective-permute-start | bytes 1572872 | tf_op jit(solution)/shard_map/ppermute | solution.py:53
  88.2 3.9 %shard_map.85 = (bf16[128,1024]{1,0:T(8,128)(2,1)}, bf16[128,2048]{1,0:T(8,128)(2,1)S(1)}, f32[128,2048]{1,0:T(8,128)S(1)}) custom-call(s32[5]{0:T(128)S(1)} %stack.23.info, bf16[512,1024]{1,0:T(8,128)(2,1)S(1)} %shard_map.78.fq, f32[512,512]{1,0:T(8,128)S(1)} %shard_map.80.y0, f32[512,512]{1,0:T(8,128)S(1)} %shard_map.82.y1, ...), custom_call_target="tpu_custom_call" | custom-call | flops 1073741824 | bytes 4194304 | tf_op jit(solution)/shard_map/pallas_call | solution.py:304
  92.1 3.9 %shard_map.84 = (bf16[128,1024]{1,0:T(8,128)(2,1)}, bf16[128,2048]{1,0:T(8,128)(2,1)S(1)}, f32[128,2048]{1,0:T(8,128)S(1)}) custom-call(s32[5]{0:T(128)S(1)} %stack.23.info, bf16[512,1024]{1,0:T(8,128)(2,1)S(1)} %shard_map.78.fq, f32[512,512]{1,0:T(8,128)S(1)} %shard_map.80.y0, f32[512,512]{1,0:T(8,128)S(1)} %shard_map.82.y1, ...), custom_call_target="tpu_custom_call" | custom-call | flops 1073741824 | bytes 4194304 | tf_op jit(solution)/shard_map/pallas_call | solution.py:304
  99.3 3.5 %collective-permute-start.15 = (bf16[128,2048]{1,0:T(8,128)(2,1)S(1)}, bf16[128,2048]{1,0:T(8,128)(2,1)S(1)}, u32[]{:S(2)}, u32[]{:S(2)}) collective-permute-start(bf16[128,2048]{1,0:T(8,128)(2,1)S(1)} %add_convert_fusion.1), channel_id=1, source_target_pairs={{0,3},{1,0},{2,1},{3,2},{4,7},{5,4},{6,5},{7,6},{8,11},{9,8},{10,9... | collective-permute-start | bytes 1572872 | tf_op jit(solution)/shard_map/ppermute | solution.py:53
  102.8 3.9 %shard_map.83 = (bf16[128,1024]{1,0:T(8,128)(2,1)}, f32[128,2048]{1,0:T(8,128)S(1)}, f32[128,2048]{1,0:T(8,128)S(1)}) custom-call(s32[5]{0:T(128)S(1)} %stack.23.info, bf16[512,1024]{1,0:T(8,128)(2,1)S(1)} %shard_map.78.fq, f32[512,512]{1,0:T(8,128)S(1)} %shard_map.80.y0, f32[512,512]{1,0:T(8,128)S(1)} %shard_map.82.y1, ...), custom_call_target="tpu_custom_call" | custom-call | flops 1073741824 | bytes 4194304 | tf_op jit(solution)/shard_map/pallas_call | solution.py:304
  106.7 3.7 %collective-permute-done.16.one = bf16[128,2048]{1,0:T(8,128)(2,1)S(1)} collective-permute-done((bf16[128,2048]{1,0:T(8,128)(2,1)S(1)}, bf16[128,2048]{1,0:T(8,128)(2,1)S(1)}, u32[]{:S(2)}, u32[]{:S(2)}) %collective-permute-start.16) | collective-permute-done | bytes 524320 | tf_op jit(solution)/shard_map/ppermute | solution.py:53
  110.4 11.0 %collective-permute-done.18.two = bf16[128,2048]{1,0:T(8,128)(2,1)S(1)} collective-permute-done((bf16[128,2048]{1,0:T(8,128)(2,1)S(1)}, bf16[128,2048]{1,0:T(8,128)(2,1)S(1)}, u32[]{:S(2)}, u32[]{:S(2)}) %collective-permute-start.18) | collective-permute-done | bytes 524320 | tf_op jit(solution)/shard_map/ppermute | solution.py:53
  (43 shorter events, 23.2 us)
Async XLA Ops:
  1.3 36.4 %collective-permute-start.5 = (bf16[512,512]{1,0:T(8,128)(2,1)S(1)}, bf16[512,512]{1,0:T(8,128)(2,1)S(1)}, u32[]{:S(2)}, u32[]{:S(2)}) collective-permute-start(bf16[512,512]{1,0:T(8,128)(2,1)S(1)} %get-tuple-element.46.refs_0_), channel_id=1, source_target_pairs={{0,3},{1,0},{2,1},{3,2},{4,7},{5,4},{6,5},{7,6},{8,11},{9,8},{10,9... | collective-permute-start | bytes 1572872 | tf_op jit(solution)/shard_map/ppermute | solution.py:53
  6.0 15.9 %collective-permute-start = (bf16[512,512]{1,0:T(8,128)(2,1)S(1)}, bf16[512,512]{1,0:T(8,128)(2,1)S(1)}, u32[]{:S(2)}, u32[]{:S(2)}) collective-permute-start(bf16[512,512]{1,0:T(8,128)(2,1)S(1)} %get-tuple-element.46.refs_0_), channel_id=1, source_target_pairs={{0,1},{1,2},{2,3},{3,0},{4,5},{5,6},{6,7},{7,4},{8,9},{9,10},{10,1... | collective-permute-start | bytes 1572872 | tf_op jit(solution)/shard_map/ppermute | solution.py:53
  6.0 31.7 %collective-permute-start.4 = (bf16[512,512]{1,0:T(8,128)(2,1)S(1)}, bf16[512,512]{1,0:T(8,128)(2,1)S(1)}, u32[]{:S(2)}, u32[]{:S(2)}) collective-permute-start(bf16[512,512]{1,0:T(8,128)(2,1)S(1)} %get-tuple-element.47.refs_1_), channel_id=1, source_target_pairs={{0,1},{1,2},{2,3},{3,0},{4,5},{5,6},{6,7},{7,4},{8,9},{9,10},{10,1... | collective-permute-start | bytes 1572872 | tf_op jit(solution)/shard_map/ppermute | solution.py:53
  6.0 21.8 %collective-permute-start.2 = (bf16[512,512]{1,0:T(8,128)(2,1)S(1)}, bf16[512,512]{1,0:T(8,128)(2,1)S(1)}, u32[]{:S(2)}, u32[]{:S(2)}) collective-permute-start(bf16[512,512]{1,0:T(8,128)(2,1)S(1)} %get-tuple-element.47.refs_1_), channel_id=1, source_target_pairs={{0,3},{1,0},{2,1},{3,2},{4,7},{5,4},{6,5},{7,6},{8,11},{9,8},{10,9... | collective-permute-start | bytes 1572872 | tf_op jit(solution)/shard_map/ppermute | solution.py:53
  21.8 22.4 %collective-permute-start.1 = (bf16[512,512]{1,0:T(8,128)(2,1)S(1)}, bf16[512,512]{1,0:T(8,128)(2,1)S(1)}, u32[]{:S(2)}, u32[]{:S(2)}) collective-permute-start(bf16[512,512]{1,0:T(8,128)(2,1)S(1)} %collective-permute-done.refs_0_), channel_id=1, source_target_pairs={{0,1},{1,2},{2,3},{3,0},{4,5},{5,6},{6,7},{7,4},{8,9},{9,10},{10,1... | collective-permute-start | bytes 1572872 | tf_op jit(solution)/shard_map/ppermute | solution.py:53
  27.8 16.4 %collective-permute-start.3 = (bf16[512,512]{1,0:T(8,128)(2,1)S(1)}, bf16[512,512]{1,0:T(8,128)(2,1)S(1)}, u32[]{:S(2)}, u32[]{:S(2)}) collective-permute-start(bf16[512,512]{1,0:T(8,128)(2,1)S(1)} %collective-permute-done.2.refs_1_), channel_id=1, source_target_pairs={{0,3},{1,0},{2,1},{3,2},{4,7},{5,4},{6,5},{7,6},{8,11},{9,8},{10,9... | collective-permute-start | bytes 1572872 | tf_op jit(solution)/shard_map/ppermute | solution.py:53
  46.6 4.3 %collective-permute-start.6 = (bf16[4,128,128]{2,1,0:T(8,128)(2,1)S(1)}, bf16[4,128,128]{2,1,0:T(8,128)(2,1)S(1)}, u32[]{:S(2)}, u32[]{:S(2)}) collective-permute-start(bf16[4,128,128]{2,1,0:T(8,128)(2,1)S(1)} %get-tuple-element.66), channel_id=1, source_target_pairs={{0,4},{4,0},{8,12},{12,8},{16,20},{20,16},{24,28},{28,24},{32,36},... | collective-permute-start | bytes 393224 | tf_op jit(solution)/shard_map/ppermute | solution.py:53
  51.0 4.2 %collective-permute-start.7 = (bf16[4,128,128]{2,1,0:T(8,128)(2,1)S(1)}, bf16[4,128,128]{2,1,0:T(8,128)(2,1)S(1)}, u32[]{:S(2)}, u32[]{:S(2)}) collective-permute-start(bf16[4,128,128]{2,1,0:T(8,128)(2,1)S(1)} %fusion.13), channel_id=1, source_target_pairs={{0,32},{4,12},{8,40},{12,4},{16,48},{20,28},{24,56},{28,20},{32,0}... | collective-permute-start | bytes 393224 | tf_op jit(solution)/shard_map/ppermute | solution.py:53
  55.2 5.4 %collective-permute-start.8 = (bf16[4,128,128]{2,1,0:T(8,128)(2,1)S(1)}, bf16[4,128,128]{2,1,0:T(8,128)(2,1)S(1)}, u32[]{:S(2)}, u32[]{:S(2)}) collective-permute-start(bf16[4,128,128]{2,1,0:T(8,128)(2,1)S(1)} %fusion.11), channel_id=1, source_target_pairs={{0,96},{4,28},{8,104},{12,20},{16,112},{20,12},{24,120},{28,4},{32... | collective-permute-start | bytes 393224 | tf_op jit(solution)/shard_map/ppermute | solution.py:53
  57.8 4.1 %collective-permute-start.10 = (bf16[4,128,128]{2,1,0:T(8,128)(2,1)S(1)}, bf16[4,128,128]{2,1,0:T(8,128)(2,1)S(1)}, u32[]{:S(2)}, u32[]{:S(2)}) collective-permute-start(bf16[4,128,128]{2,1,0:T(8,128)(2,1)S(1)} %fusion.13), channel_id=1, source_target_pairs={{0,8},{4,36},{8,0},{12,44},{16,24},{20,52},{24,16},{28,60},{32,40}... | collective-permute-start | bytes 393224 | tf_op jit(solution)/shard_map/ppermute | solution.py:53
  60.8 3.9 %collective-permute-start.9 = (bf16[4,128,128]{2,1,0:T(8,128)(2,1)S(1)}, bf16[4,128,128]{2,1,0:T(8,128)(2,1)S(1)}, u32[]{:S(2)}, u32[]{:S(2)}) collective-permute-start(bf16[4,128,128]{2,1,0:T(8,128)(2,1)S(1)} %fusion.12), channel_id=1, source_target_pairs={{0,8},{4,36},{8,0},{12,44},{16,24},{20,52},{24,16},{28,60},{32,40}... | collective-permute-start | bytes 393224 | tf_op jit(solution)/shard_map/ppermute | solution.py:53
  64.8 5.2 %collective-permute-start.11 = (bf16[4,128,128]{2,1,0:T(8,128)(2,1)S(1)}, bf16[4,128,128]{2,1,0:T(8,128)(2,1)S(1)}, u32[]{:S(2)}, u32[]{:S(2)}) collective-permute-start(bf16[4,128,128]{2,1,0:T(8,128)(2,1)S(1)} %fusion.9), channel_id=1, source_target_pairs={{0,24},{4,100},{8,16},{12,108},{16,8},{20,116},{24,0},{28,124},{32... | collective-permute-start | bytes 393224 | tf_op jit(solution)/shard_map/ppermute | solution.py:53
  70.2 11.4 %collective-permute-start.12 = (bf16[4,128,128]{2,1,0:T(8,128)(2,1)S(1)}, bf16[4,128,128]{2,1,0:T(8,128)(2,1)S(1)}, u32[]{:S(2)}, u32[]{:S(2)}) collective-permute-start(bf16[4,128,128]{2,1,0:T(8,128)(2,1)S(1)} %get-tuple-element.83), channel_id=1, source_target_pairs={{0,4},{4,0},{8,12},{12,8},{16,20},{20,16},{24,28},{28,24},{32,36},... | collective-permute-start | bytes 393224 | tf_op jit(solution)/shard_map/ppermute | solution.py:53
  78.9 2.8 %copy-start = (f32[1024]{0:T(1024)S(1)}, f32[1024]{0:T(1024)}, u32[]{:S(2)}) copy-start(f32[1024]{0:T(1024)} %param.12) | copy-start | bytes 12292
  83.9 14.9 %collective-permute-start.17 = (bf16[128,2048]{1,0:T(8,128)(2,1)S(1)}, bf16[128,2048]{1,0:T(8,128)(2,1)S(1)}, u32[]{:S(2)}, u32[]{:S(2)}) collective-permute-start(bf16[128,2048]{1,0:T(8,128)(2,1)S(1)} %get-tuple-element.82), channel_id=1, source_target_pairs={{0,1},{1,2},{2,3},{3,0},{4,5},{5,6},{6,7},{7,4},{8,9},{9,10},{10,1... | collective-permute-start | bytes 1572872 | tf_op jit(solution)/shard_map/ppermute | solution.py:53
  85.4 13.7 %collective-permute-start.14 = (bf16[128,2048]{1,0:T(8,128)(2,1)S(1)}, bf16[128,2048]{1,0:T(8,128)(2,1)S(1)}, u32[]{:S(2)}, u32[]{:S(2)}) collective-permute-start(bf16[128,2048]{1,0:T(8,128)(2,1)S(1)} %shard_map.87), channel_id=1, source_target_pairs={{0,3},{1,0},{2,1},{3,2},{4,7},{5,4},{6,5},{7,6},{8,11},{9,8},{10,9... | collective-permute-start | bytes 1572872 | tf_op jit(solution)/shard_map/ppermute | solution.py:53
  92.1 18.3 %collective-permute-start.16 = (bf16[128,2048]{1,0:T(8,128)(2,1)S(1)}, bf16[128,2048]{1,0:T(8,128)(2,1)S(1)}, u32[]{:S(2)}, u32[]{:S(2)}) collective-permute-start(bf16[128,2048]{1,0:T(8,128)(2,1)S(1)} %get-tuple-element.80), channel_id=1, source_target_pairs={{0,3},{1,0},{2,1},{3,2},{4,7},{5,4},{6,5},{7,6},{8,11},{9,8},{10,9... | collective-permute-start | bytes 1572872 | tf_op jit(solution)/shard_map/ppermute | solution.py:53
  96.1 26.4 %collective-permute-start.13 = (bf16[128,2048]{1,0:T(8,128)(2,1)S(1)}, bf16[128,2048]{1,0:T(8,128)(2,1)S(1)}, u32[]{:S(2)}, u32[]{:S(2)}) collective-permute-start(bf16[128,2048]{1,0:T(8,128)(2,1)S(1)} %get-tuple-element.76), channel_id=1, source_target_pairs={{0,1},{1,2},{2,3},{3,0},{4,5},{5,6},{6,7},{7,4},{8,9},{9,10},{10,1... | collective-permute-start | bytes 1572872 | tf_op jit(solution)/shard_map/ppermute | solution.py:53
  99.0 22.5 %collective-permute-start.18 = (bf16[128,2048]{1,0:T(8,128)(2,1)S(1)}, bf16[128,2048]{1,0:T(8,128)(2,1)S(1)}, u32[]{:S(2)}, u32[]{:S(2)}) collective-permute-start(bf16[128,2048]{1,0:T(8,128)(2,1)S(1)} %add_convert_fusion), channel_id=1, source_target_pairs={{0,1},{1,2},{2,3},{3,0},{4,5},{5,6},{6,7},{7,4},{8,9},{9,10},{10,1... | collective-permute-start | bytes 1572872 | tf_op jit(solution)/shard_map/ppermute | solution.py:53
  99.3 23.1 %collective-permute-start.15 = (bf16[128,2048]{1,0:T(8,128)(2,1)S(1)}, bf16[128,2048]{1,0:T(8,128)(2,1)S(1)}, u32[]{:S(2)}, u32[]{:S(2)}) collective-permute-start(bf16[128,2048]{1,0:T(8,128)(2,1)S(1)} %add_convert_fusion.1), channel_id=1, source_target_pairs={{0,3},{1,0},{2,1},{3,2},{4,7},{5,4},{6,5},{7,6},{8,11},{9,8},{10,9... | collective-permute-start | bytes 1572872 | tf_op jit(solution)/shard_map/ppermute | solution.py:53

commit v3 on v2

--- a/solution.py
+++ b/solution.py
@@ -27,26 +27,18 @@
     return (y * 4 + x) * 2 + c
 
 
-def exchange(move, first):
+def turn(k, first):
     found = []
     for y in range(4):
         for x in range(4):
             for c in range(2):
                 along_y = (c == 0) == first
-                to = (move(y), x, c) if along_y else (y, move(x), c)
+                to = ((y + k) % 4, x, c) if along_y else (y, (x + k) % 4, c)
                 found.append((chip(y, x, c), chip(*to)))
     return found
 
 
 SWAP = [(s, s ^ 1) for s in range(32)]
-
-
-def near(v):
-    return v ^ 1
-
-
-def mirror(v):
-    return 3 - v
 
 
 def shift(v, pairs, axis="tp"):
@@ -354,23 +346,18 @@
 
 
 def before_this(flags, mine, other):
-    core0, core1, odd_a, high_a, first_low, early_t, early_p, all_p = flags
+    core0, core1, seen_a, later_b, seen_b = flags[0], flags[1], flags[2:5], flags[5:8], flags[8:]
 
     def send(v, pairs):
         return shift(v.astype(bf16), pairs, "seq").astype(f32)
 
     theirs = send(other, SWAP)
     both = mine + theirs
-    r1 = send(both, exchange(near, True))
-    two = both + r1
-    r2 = send(two, exchange(mirror, True))
-    t3 = send(both, exchange(near, False))
-    earlier = odd_a * r1 + high_a * r2
-    first = core0 * earlier + core1 * (two + r2)
-    r3 = send(first, exchange(near, False))
-    v = first + r3 + first_low * (both + t3)
-    r4 = send(v, exchange(mirror, False))
-    prefix = earlier + early_p * r3 + early_t * t3 + all_p * r4
+    r = {k: send(both, turn(k, True)) for k in (2, 1, 3)}
+    earlier = seen_a[0] * r[1] + seen_a[1] * r[2] + seen_a[2] * r[3]
+    total = core0 * earlier + core1 * (both + r[1] + r[2] + r[3])
+    t = {k: send(total + later_b[k - 1] * both, turn(k, False)) for k in (2, 1, 3)}
+    prefix = earlier + seen_b[0] * t[1] + seen_b[1] * t[2] + seen_b[2] * t[3]
     own = (prefix + core1 * theirs).astype(bf16)
     return own, send(prefix + core0 * mine, SWAP).astype(bf16)
 
@@ -382,19 +369,11 @@
     first, second = jnp.where(core == 0, y, x), jnp.where(core == 0, x, y)
     info = jnp.stack([z, (z + 3) % 4, (z + 1) % 4, (z + 2) % 4, 1 - core]).astype(jnp.int32)
     core0, core1 = core == 0, core == 1
-    flags = [
-        v.astype(f32)
-        for v in (
-            core0,
-            core1,
-            first % 2,
-            first // 2,
-            core0 & (second < 2),
-            core0 & (second % 2 == 1),
-            core0 | (second % 2 == 1),
-            core0 | (second >= 2),
-        )
-    ]
+    flags = [core0, core1]
+    flags += [first >= k for k in (1, 2, 3)]
+    flags += [core0 & (second < 4 - k) for k in (1, 2, 3)]
+    flags += [core0 | (second >= k) for k in (1, 2, 3)]
+    flags = [v.astype(f32) for v in flags]
     _, part = codes.shape
     width = w_query.shape[1]
     half = w_out.shape[1] // 2

time: 124 us -> 119 us (0.960)
  waiting for transfers between devices: 31.7 us -> 28.6 us
  starting transfers between devices: 33.8 us -> 31.6 us
    ppermute x19 -> x20, waiting for transfers between devices: 31.7 us -> 28.6 us  [shift(): return lax.ppermute(v, axis, pairs)]
    ppermute x19 -> x20, starting transfers between devices: 33.8 us -> 31.6 us  [shift(): return lax.ppermute(v, axis, pairs)]
  transfers between devices with their start and end apart: 19 -> 20, of which waited for: 10 -> 9; matrix products, arithmetic and copies ran while one was open for 1% -> 1% of each run, Pallas kernels for 40% -> 42%
where the time goes in v3:
time: 119 us; the launch traced here: 118 us
  Pallas kernels  55.9 us (47%)
  starting transfers between devices  31.6 us (27%)
  waiting for transfers between devices  28.6 us (24%)
  other arithmetic  1.43 us (1%)
    ppermute x20, starting transfers between devices, shift(): return lax.ppermute(v, axis, pairs)  31.6 us
    ppermute x20, waiting for transfers between devices, shift(): return lax.ppermute(v, axis, pairs)  28.6 us
    pallas_call x3, Pallas kernels, project(): pl.pallas_call(functools.partial(project_kernel, count, have), out_shape=...  19.4 us
    pallas_call x4, Pallas kernels, first_share(): pl.pallas_call(functools.partial(first_kernel, place, spans), out_shape=[...  14 us
    pallas_call x1, Pallas kernels, fetch(): pl.pallas_call(functools.partial(fetch_kernel, rows), out_shape=[pltpu.VM...  5.84 us
    pallas_call x2, Pallas kernels, within(): pl.pallas_call(functools.partial(within_kernel, part), out_shape=pltpu.VM...  5.49 us
    pallas_call x2, Pallas kernels, last_kv(): pl.pallas_call(functools.partial(last_kv_kernel, part), out_shape=[pltpu....  4.83 us
  transfers between devices with their start and end apart: 20, of which 9 were waited for; matrix products, arithmetic and copies ran while one was open for 1% of the time, Pallas kernels for 42%

profile of v3, /device:TPU:1, one launch (start us, length us, event | category | flops | bytes accessed | tf_op | source)
XLA Modules:
  0.0 118.1 jit_solution(2309482678388693674)
XLA Ops:
  1.3 4.6 %collective-permute-start.5 = (bf16[512,512]{1,0:T(8,128)(2,1)S(1)}, bf16[512,512]{1,0:T(8,128)(2,1)S(1)}, u32[]{:S(2)}, u32[]{:S(2)}) collective-permute-start(bf16[512,512]{1,0:T(8,128)(2,1)S(1)} %get-tuple-element.49.refs_0_), channel_id=1, source_target_pairs={{0,3},{1,0},{2,1},{3,2},{4,7},{5,4},{6,5},{7,6},{8,11},{9,8},{10,9... | collective-permute-start | bytes 1572872 | tf_op jit(solution)/shard_map/ppermute | solution.py:45
  6.0 2.7 %collective-permute-start.2 = (bf16[512,512]{1,0:T(8,128)(2,1)S(1)}, bf16[512,512]{1,0:T(8,128)(2,1)S(1)}, u32[]{:S(2)}, u32[]{:S(2)}) collective-permute-start(bf16[512,512]{1,0:T(8,128)(2,1)S(1)} %get-tuple-element.50.refs_1_), channel_id=1, source_target_pairs={{0,3},{1,0},{2,1},{3,2},{4,7},{5,4},{6,5},{7,6},{8,11},{9,8},{10,9... | collective-permute-start | bytes 1572872 | tf_op jit(solution)/shard_map/ppermute | solution.py:45
  9.5 5.8 %shard_map.74 = (bf16[1024,1024]{1,0:T(8,128)(2,1)S(1)}, bf16[1024,1024]{1,0:T(8,128)(2,1)S(1)}, bf16[1024,1024]{1,0:T(8,128)(2,1)S(1)}, bf16[1024,4096]{1,0:T(8,128)(2,1)S(1)}) custom-call(s32[5]{0:T(128)S(1)} %stack.23.info, bf16[4096,1024]{1,0:T(8,128)(2,1)} %refs_5_.5, bf16[4096,1024]{1,0:T(8,128)(2,1)} %refs_6_.5, bf16[4096,1024]{1,0:T(8,128)(2,1)} %refs_7_.5, ...), custom_call_target="tpu_custom_call" | custom-call | bytes 14680064 | tf_op jit(solution)/shard_map/pallas_call | solution.py:146
  15.3 6.5 %shard_map.75 = (f32[512,1024]{1,0:T(8,128)S(1)}, f32[512,1024]{1,0:T(8,128)S(1)}, f32[512,1024]{1,0:T(8,128)S(1)}) custom-call(s32[5]{0:T(128)S(1)} %stack.23.info, bf16[512,512]{1,0:T(8,128)(2,1)S(1)} %get-tuple-element.49.refs_0_, bf16[512,512]{1,0:T(8,128)(2,1)S(1)} %get-tuple-element.50.refs_1_, bf16[4096,1024]{1,0:T(8,128)(2,1)} %refs_5_.5, ...), custom_call_target="tpu_custom_call" | custom-call | flops 3221225472 | bytes 6291456 | tf_op jit(solution)/shard_map/pallas_call | solution.py:90
  21.9 5.9 %collective-permute-done.2.refs_1_ = bf16[512,512]{1,0:T(8,128)(2,1)S(1)} collective-permute-done((bf16[512,512]{1,0:T(8,128)(2,1)S(1)}, bf16[512,512]{1,0:T(8,128)(2,1)S(1)}, u32[]{:S(2)}, u32[]{:S(2)}) %collective-permute-start.2) | collective-permute-done | bytes 524320 | tf_op jit(solution)/shard_map/ppermute | solution.py:45
  27.8 3.4 %collective-permute-start.3 = (bf16[512,512]{1,0:T(8,128)(2,1)S(1)}, bf16[512,512]{1,0:T(8,128)(2,1)S(1)}, u32[]{:S(2)}, u32[]{:S(2)}) collective-permute-start(bf16[512,512]{1,0:T(8,128)(2,1)S(1)} %collective-permute-done.2.refs_1_), channel_id=1, source_target_pairs={{0,3},{1,0},{2,1},{3,2},{4,7},{5,4},{6,5},{7,6},{8,11},{9,8},{10,9... | collective-permute-start | bytes 1572872 | tf_op jit(solution)/shard_map/ppermute | solution.py:45
  31.2 6.5 %shard_map.76 = (f32[512,1024]{1,0:T(8,128)S(1)}, f32[512,1024]{1,0:T(8,128)S(1)}, f32[512,1024]{1,0:T(8,128)S(1)}) custom-call(s32[5]{0:T(128)S(1)} %stack.23.info, bf16[512,512]{1,0:T(8,128)(2,1)S(1)} %collective-permute-done.refs_0_, bf16[512,512]{1,0:T(8,128)(2,1)S(1)} %collective-permute-done.2.refs_1_, bf16[4096,1024]{1,0:T(8,128)(2,1)} %refs_5_.5, ...), custom_call_target="tpu_custom_call" | custom-call | flops 3221225472 | bytes 6291456 | tf_op jit(solution)/shard_map/pallas_call | solution.py:90
  37.7 6.5 %shard_map.77 = (f32[512,1024]{1,0:T(8,128)S(1)}, f32[512,1024]{1,0:T(8,128)S(1)}, f32[512,1024]{1,0:T(8,128)S(1)}) custom-call(s32[5]{0:T(128)S(1)} %stack.23.info, bf16[512,512]{1,0:T(8,128)(2,1)S(1)} %collective-permute-done.4.refs_0_, bf16[512,512]{1,0:T(8,128)(2,1)S(1)} %collective-permute-done.5.refs_1_, bf16[4096,1024]{1,0:T(8,128)(2,1)} %refs_5_.5, ...), custom_call_target="tpu_custom_call" | custom-call | flops 3221225472 | bytes 6291456 | tf_op jit(solution)/shard_map/pallas_call | solution.py:90
  44.2 2.4 %shard_map.81 = (bf16[512,512]{1,0:T(8,128)(2,1)S(1)}, bf16[512,512]{1,0:T(8,128)(2,1)S(1)}, bf16[4,128,128]{2,1,0:T(8,128)(2,1)S(1)}) custom-call(s32[5]{0:T(128)S(1)} %stack.23.info, bf16[512,512]{1,0:T(8,128)(2,1)S(1)} %collective-permute-done.1.xa, bf16[512,512]{1,0:T(8,128)(2,1)S(1)} %collective-permute-done.3.xb, ...), custom_call_target="tpu_custom_call" | custom-call | flops 1073741824 | bytes 4194304 | tf_op jit(solution)/shard_map/pallas_call | solution.py:187
  48.5 2.4 %shard_map.79 = (bf16[512,512]{1,0:T(8,128)(2,1)S(1)}, bf16[512,512]{1,0:T(8,128)(2,1)S(1)}, f32[4,128,128]{2,1,0:T(8,128)S(1)}) custom-call(s32[5]{0:T(128)S(1)} %stack.23.info, bf16[512,512]{1,0:T(8,128)(2,1)S(1)} %collective-permute-done.1.xa, bf16[512,512]{1,0:T(8,128)(2,1)S(1)} %collective-permute-done.3.xb, ...), custom_call_target="tpu_custom_call" | custom-call | flops 1073741824 | bytes 4194304 | tf_op jit(solution)/shard_map/pallas_call | solution.py:187
  51.0 2.5 %collective-permute-start.9 = (bf16[4,128,128]{2,1,0:T(8,128)(2,1)S(1)}, bf16[4,128,128]{2,1,0:T(8,128)(2,1)S(1)}, u32[]{:S(2)}, u32[]{:S(2)}) collective-permute-start(bf16[4,128,128]{2,1,0:T(8,128)(2,1)S(1)} %fusion.6), channel_id=1, source_target_pairs={{0,96},{4,28},{8,104},{12,4},{16,112},{20,12},{24,120},{28,20},{32... | collective-permute-start | bytes 393224 | tf_op jit(solution)/shard_map/ppermute | solution.py:45
  56.9 2.3 %collective-permute-done.8 = bf16[4,128,128]{2,1,0:T(8,128)(2,1)S(1)} collective-permute-done((bf16[4,128,128]{2,1,0:T(8,128)(2,1)S(1)}, bf16[4,128,128]{2,1,0:T(8,128)(2,1)S(1)}, u32[]{:S(2)}, u32[]{:S(2)}) %collective-permute-start.8) | collective-permute-done | bytes 131104 | tf_op jit(solution)/shard_map/ppermute | solution.py:45
  61.9 2.6 %collective-permute-start.11 = (bf16[4,128,128]{2,1,0:T(8,128)(2,1)S(1)}, bf16[4,128,128]{2,1,0:T(8,128)(2,1)S(1)}, u32[]{:S(2)}, u32[]{:S(2)}) collective-permute-start(bf16[4,128,128]{2,1,0:T(8,128)(2,1)S(1)} %get-tuple-element.92), channel_id=1, source_target_pairs={{0,16},{4,68},{8,24},{12,76},{16,0},{20,84},{24,8},{28,92},{32,48}... | collective-permute-start | bytes 393224 | tf_op jit(solution)/shard_map/ppermute | solution.py:45
  67.4 2.7 %shard_map.80.y0 = f32[512,512]{1,0:T(8,128)S(1)} custom-call(s32[5]{0:T(128)S(1)} %stack.23.info, bf16[512,1024]{1,0:T(8,128)(2,1)S(1)} %shard_map.78.fq, bf16[512,512]{1,0:T(8,128)(2,1)S(1)} %get-tuple-element.63.fk, bf16[512,512]{1,0:T(8,128)(2,1)S(1)} %get-tuple-element.64.vb), custom_call_target="tpu_custom_call" | custom-call | flops 536870912 | bytes 4194304 | tf_op jit(solution)/shard_map/pallas_call | solution.py:255
  70.2 2.7 %shard_map.82.y1 = f32[512,512]{1,0:T(8,128)S(1)} custom-call(s32[5]{0:T(128)S(1)} %stack.23.info, bf16[512,1024]{1,0:T(8,128)(2,1)S(1)} %shard_map.78.fq, bf16[512,512]{1,0:T(8,128)(2,1)S(1)} %get-tuple-element.65.fk, bf16[512,512]{1,0:T(8,128)(2,1)S(1)} %get-tuple-element.66.vb), custom_call_target="tpu_custom_call" | custom-call | flops 536870912 | bytes 4194304 | tf_op jit(solution)/shard_map/pallas_call | solution.py:255
  73.1 2.7 %collective-permute-start.13 = (bf16[4,128,128]{2,1,0:T(8,128)(2,1)S(1)}, bf16[4,128,128]{2,1,0:T(8,128)(2,1)S(1)}, u32[]{:S(2)}, u32[]{:S(2)}) collective-permute-start(bf16[4,128,128]{2,1,0:T(8,128)(2,1)S(1)} %get-tuple-element.89), channel_id=1, source_target_pairs={{0,4},{4,0},{8,12},{12,8},{16,20},{20,16},{24,28},{28,24},{32,36},... | collective-permute-start | bytes 393224 | tf_op jit(solution)/shard_map/ppermute | solution.py:45
  76.8 2.2 %shard_map.86 = (bf16[128,1024]{1,0:T(8,128)(2,1)S(1)}, bf16[128,2048]{1,0:T(8,128)(2,1)S(1)}) custom-call(s32[5]{0:T(128)S(1)} %stack.23.info, bf16[512,1024]{1,0:T(8,128)(2,1)S(1)} %shard_map.78.fq, f32[512,512]{1,0:T(8,128)S(1)} %shard_map.80.y0, f32[512,512]{1,0:T(8,128)S(1)} %shard_map.82.y1, bf16[4,128,128]{2,1,0:T(8,128)(2,1)S(1)} %fusion.1.own, ...), custom_call_target="tpu_custom_call" | custom-call | flops 536870912 | bytes 4194304 | tf_op jit(solution)/shard_map/pallas_call | solution.py:296
  80.4 2.7 %collective-permute-start.15 = (bf16[128,2048]{1,0:T(8,128)(2,1)S(1)}, bf16[128,2048]{1,0:T(8,128)(2,1)S(1)}, u32[]{:S(2)}, u32[]{:S(2)}) collective-permute-start(bf16[128,2048]{1,0:T(8,128)(2,1)S(1)} %shard_map.87), channel_id=1, source_target_pairs={{0,3},{1,0},{2,1},{3,2},{4,7},{5,4},{6,5},{7,6},{8,11},{9,8},{10,9... | collective-permute-start | bytes 1572872 | tf_op jit(solution)/shard_map/ppermute | solution.py:45
  83.1 3.9 %shard_map.85 = (bf16[128,1024]{1,0:T(8,128)(2,1)}, bf16[128,2048]{1,0:T(8,128)(2,1)S(1)}, f32[128,2048]{1,0:T(8,128)S(1)}) custom-call(s32[5]{0:T(128)S(1)} %stack.23.info, bf16[512,1024]{1,0:T(8,128)(2,1)S(1)} %shard_map.78.fq, f32[512,512]{1,0:T(8,128)S(1)} %shard_map.80.y0, f32[512,512]{1,0:T(8,128)S(1)} %shard_map.82.y1, ...), custom_call_target="tpu_custom_call" | custom-call | flops 1073741824 | bytes 4194304 | tf_op jit(solution)/shard_map/pallas_call | solution.py:296
  87.1 3.9 %shard_map.84 = (bf16[128,1024]{1,0:T(8,128)(2,1)}, bf16[128,2048]{1,0:T(8,128)(2,1)S(1)}, f32[128,2048]{1,0:T(8,128)S(1)}) custom-call(s32[5]{0:T(128)S(1)} %stack.23.info, bf16[512,1024]{1,0:T(8,128)(2,1)S(1)} %shard_map.78.fq, f32[512,512]{1,0:T(8,128)S(1)} %shard_map.80.y0, f32[512,512]{1,0:T(8,128)S(1)} %shard_map.82.y1, ...), custom_call_target="tpu_custom_call" | custom-call | flops 1073741824 | bytes 4194304 | tf_op jit(solution)/shard_map/pallas_call | solution.py:296
  93.9 3.5 %collective-permute-start.16 = (bf16[128,2048]{1,0:T(8,128)(2,1)S(1)}, bf16[128,2048]{1,0:T(8,128)(2,1)S(1)}, u32[]{:S(2)}, u32[]{:S(2)}) collective-permute-start(bf16[128,2048]{1,0:T(8,128)(2,1)S(1)} %add_convert_fusion.1), channel_id=1, source_target_pairs={{0,3},{1,0},{2,1},{3,2},{4,7},{5,4},{6,5},{7,6},{8,11},{9,8},{10,9... | collective-permute-start | bytes 1572872 | tf_op jit(solution)/shard_map/ppermute | solution.py:45
  97.4 3.9 %shard_map.83 = (bf16[128,1024]{1,0:T(8,128)(2,1)}, f32[128,2048]{1,0:T(8,128)S(1)}, f32[128,2048]{1,0:T(8,128)S(1)}) custom-call(s32[5]{0:T(128)S(1)} %stack.23.info, bf16[512,1024]{1,0:T(8,128)(2,1)S(1)} %shard_map.78.fq, f32[512,512]{1,0:T(8,128)S(1)} %shard_map.80.y0, f32[512,512]{1,0:T(8,128)S(1)} %shard_map.82.y1, bf16[4,128,128]{2,1,0:T(8,128)(2,1)S(1)} %fusion.1.own, ...), custom_call_target="tpu_custom_call" | custom-call | flops 1073741824 | bytes 4194304 | tf_op jit(solution)/shard_map/pallas_call | solution.py:296
  101.3 3.7 %collective-permute-done.17.one = bf16[128,2048]{1,0:T(8,128)(2,1)S(1)} collective-permute-done((bf16[128,2048]{1,0:T(8,128)(2,1)S(1)}, bf16[128,2048]{1,0:T(8,128)(2,1)S(1)}, u32[]{:S(2)}, u32[]{:S(2)}) %collective-permute-start.17) | collective-permute-done | bytes 524320 | tf_op jit(solution)/shard_map/ppermute | solution.py:45
  105.0 11.0 %collective-permute-done.19.two = bf16[128,2048]{1,0:T(8,128)(2,1)S(1)} collective-permute-done((bf16[128,2048]{1,0:T(8,128)(2,1)S(1)}, bf16[128,2048]{1,0:T(8,128)(2,1)S(1)}, u32[]{:S(2)}, u32[]{:S(2)}) %collective-permute-start.19) | collective-permute-done | bytes 524320 | tf_op jit(solution)/shard_map/ppermute | solution.py:45
  (44 shorter events, 20.5 us)
Async XLA Ops:
  1.3 36.4 %collective-permute-start.5 = (bf16[512,512]{1,0:T(8,128)(2,1)S(1)}, bf16[512,512]{1,0:T(8,128)(2,1)S(1)}, u32[]{:S(2)}, u32[]{:S(2)}) collective-permute-start(bf16[512,512]{1,0:T(8,128)(2,1)S(1)} %get-tuple-element.49.refs_0_), channel_id=1, source_target_pairs={{0,3},{1,0},{2,1},{3,2},{4,7},{5,4},{6,5},{7,6},{8,11},{9,8},{10,9... | collective-permute-start | bytes 1572872 | tf_op jit(solution)/shard_map/ppermute | solution.py:45
  6.0 15.9 %collective-permute-start = (bf16[512,512]{1,0:T(8,128)(2,1)S(1)}, bf16[512,512]{1,0:T(8,128)(2,1)S(1)}, u32[]{:S(2)}, u32[]{:S(2)}) collective-permute-start(bf16[512,512]{1,0:T(8,128)(2,1)S(1)} %get-tuple-element.49.refs_0_), channel_id=1, source_target_pairs={{0,1},{1,2},{2,3},{3,0},{4,5},{5,6},{6,7},{7,4},{8,9},{9,10},{10,1... | collective-permute-start | bytes 1572872 | tf_op jit(solution)/shard_map/ppermute | solution.py:45
  6.0 31.7 %collective-permute-start.4 = (bf16[512,512]{1,0:T(8,128)(2,1)S(1)}, bf16[512,512]{1,0:T(8,128)(2,1)S(1)}, u32[]{:S(2)}, u32[]{:S(2)}) collective-permute-start(bf16[512,512]{1,0:T(8,128)(2,1)S(1)} %get-tuple-element.50.refs_1_), channel_id=1, source_target_pairs={{0,1},{1,2},{2,3},{3,0},{4,5},{5,6},{6,7},{7,4},{8,9},{9,10},{10,1... | collective-permute-start | bytes 1572872 | tf_op jit(solution)/shard_map/ppermute | solution.py:45
  6.0 21.8 %collective-permute-start.2 = (bf16[512,512]{1,0:T(8,128)(2,1)S(1)}, bf16[512,512]{1,0:T(8,128)(2,1)S(1)}, u32[]{:S(2)}, u32[]{:S(2)}) collective-permute-start(bf16[512,512]{1,0:T(8,128)(2,1)S(1)} %get-tuple-element.50.refs_1_), channel_id=1, source_target_pairs={{0,3},{1,0},{2,1},{3,2},{4,7},{5,4},{6,5},{7,6},{8,11},{9,8},{10,9... | collective-permute-start | bytes 1572872 | tf_op jit(solution)/shard_map/ppermute | solution.py:45
  21.8 22.4 %collective-permute-start.1 = (bf16[512,512]{1,0:T(8,128)(2,1)S(1)}, bf16[512,512]{1,0:T(8,128)(2,1)S(1)}, u32[]{:S(2)}, u32[]{:S(2)}) collective-permute-start(bf16[512,512]{1,0:T(8,128)(2,1)S(1)} %collective-permute-done.refs_0_), channel_id=1, source_target_pairs={{0,1},{1,2},{2,3},{3,0},{4,5},{5,6},{6,7},{7,4},{8,9},{9,10},{10,1... | collective-permute-start | bytes 1572872 | tf_op jit(solution)/shard_map/ppermute | solution.py:45
  27.8 16.4 %collective-permute-start.3 = (bf16[512,512]{1,0:T(8,128)(2,1)S(1)}, bf16[512,512]{1,0:T(8,128)(2,1)S(1)}, u32[]{:S(2)}, u32[]{:S(2)}) collective-permute-start(bf16[512,512]{1,0:T(8,128)(2,1)S(1)} %collective-permute-done.2.refs_1_), channel_id=1, source_target_pairs={{0,3},{1,0},{2,1},{3,2},{4,7},{5,4},{6,5},{7,6},{8,11},{9,8},{10,9... | collective-permute-start | bytes 1572872 | tf_op jit(solution)/shard_map/ppermute | solution.py:45
  46.6 4.3 %collective-permute-start.6 = (bf16[4,128,128]{2,1,0:T(8,128)(2,1)S(1)}, bf16[4,128,128]{2,1,0:T(8,128)(2,1)S(1)}, u32[]{:S(2)}, u32[]{:S(2)}) collective-permute-start(bf16[4,128,128]{2,1,0:T(8,128)(2,1)S(1)} %get-tuple-element.69), channel_id=1, source_target_pairs={{0,4},{4,0},{8,12},{12,8},{16,20},{20,16},{24,28},{28,24},{32,36},... | collective-permute-start | bytes 393224 | tf_op jit(solution)/shard_map/ppermute | solution.py:45
  51.0 5.9 %collective-permute-start.9 = (bf16[4,128,128]{2,1,0:T(8,128)(2,1)S(1)}, bf16[4,128,128]{2,1,0:T(8,128)(2,1)S(1)}, u32[]{:S(2)}, u32[]{:S(2)}) collective-permute-start(bf16[4,128,128]{2,1,0:T(8,128)(2,1)S(1)} %fusion.6), channel_id=1, source_target_pairs={{0,96},{4,28},{8,104},{12,4},{16,112},{20,12},{24,120},{28,20},{32... | collective-permute-start | bytes 393224 | tf_op jit(solution)/shard_map/ppermute | solution.py:45
  53.5 5.6 %collective-permute-start.8 = (bf16[4,128,128]{2,1,0:T(8,128)(2,1)S(1)}, bf16[4,128,128]{2,1,0:T(8,128)(2,1)S(1)}, u32[]{:S(2)}, u32[]{:S(2)}) collective-permute-start(bf16[4,128,128]{2,1,0:T(8,128)(2,1)S(1)} %fusion.6), channel_id=1, source_target_pairs={{0,64},{4,20},{8,72},{12,28},{16,80},{20,4},{24,88},{28,12},{32,96... | collective-permute-start | bytes 393224 | tf_op jit(solution)/shard_map/ppermute | solution.py:45
  54.1 6.5 %collective-permute-start.7 = (bf16[4,128,128]{2,1,0:T(8,128)(2,1)S(1)}, bf16[4,128,128]{2,1,0:T(8,128)(2,1)S(1)}, u32[]{:S(2)}, u32[]{:S(2)}) collective-permute-start(bf16[4,128,128]{2,1,0:T(8,128)(2,1)S(1)} %fusion.6), channel_id=1, source_target_pairs={{0,32},{4,12},{8,40},{12,20},{16,48},{20,28},{24,56},{28,4},{32,64... | collective-permute-start | bytes 393224 | tf_op jit(solution)/shard_map/ppermute | solution.py:45
  60.8 12.1 %collective-permute-start.10 = (bf16[4,128,128]{2,1,0:T(8,128)(2,1)S(1)}, bf16[4,128,128]{2,1,0:T(8,128)(2,1)S(1)}, u32[]{:S(2)}, u32[]{:S(2)}) collective-permute-start(bf16[4,128,128]{2,1,0:T(8,128)(2,1)S(1)} %get-tuple-element.91), channel_id=1, source_target_pairs={{0,8},{4,36},{8,16},{12,44},{16,24},{20,52},{24,0},{28,60},{32,40}... | collective-permute-start | bytes 393224 | tf_op jit(solution)/shard_map/ppermute | solution.py:45
  61.9 11.1 %collective-permute-start.11 = (bf16[4,128,128]{2,1,0:T(8,128)(2,1)S(1)}, bf16[4,128,128]{2,1,0:T(8,128)(2,1)S(1)}, u32[]{:S(2)}, u32[]{:S(2)}) collective-permute-start(bf16[4,128,128]{2,1,0:T(8,128)(2,1)S(1)} %get-tuple-element.92), channel_id=1, source_target_pairs={{0,16},{4,68},{8,24},{12,76},{16,0},{20,84},{24,8},{28,92},{32,48}... | collective-permute-start | bytes 393224 | tf_op jit(solution)/shard_map/ppermute | solution.py:45
  64.5 8.5 %collective-permute-start.12 = (bf16[4,128,128]{2,1,0:T(8,128)(2,1)S(1)}, bf16[4,128,128]{2,1,0:T(8,128)(2,1)S(1)}, u32[]{:S(2)}, u32[]{:S(2)}) collective-permute-start(bf16[4,128,128]{2,1,0:T(8,128)(2,1)S(1)} %get-tuple-element.93), channel_id=1, source_target_pairs={{0,24},{4,100},{8,0},{12,108},{16,8},{20,116},{24,16},{28,124},{32... | collective-permute-start | bytes 393224 | tf_op jit(solution)/shard_map/ppermute | solution.py:45
  70.2 6.6 %copy-start = (f32[1024]{0:T(1024)S(1)}, f32[1024]{0:T(1024)}, u32[]{:S(2)}) copy-start(f32[1024]{0:T(1024)} %param.12) | copy-start | bytes 12292
  73.1 3.6 %collective-permute-start.13 = (bf16[4,128,128]{2,1,0:T(8,128)(2,1)S(1)}, bf16[4,128,128]{2,1,0:T(8,128)(2,1)S(1)}, u32[]{:S(2)}, u32[]{:S(2)}) collective-permute-start(bf16[4,128,128]{2,1,0:T(8,128)(2,1)S(1)} %get-tuple-element.89), channel_id=1, source_target_pairs={{0,4},{4,0},{8,12},{12,8},{16,20},{20,16},{24,28},{28,24},{32,36},... | collective-permute-start | bytes 393224 | tf_op jit(solution)/shard_map/ppermute | solution.py:45
  79.0 14.4 %collective-permute-start.18 = (bf16[128,2048]{1,0:T(8,128)(2,1)S(1)}, bf16[128,2048]{1,0:T(8,128)(2,1)S(1)}, u32[]{:S(2)}, u32[]{:S(2)}) collective-permute-start(bf16[128,2048]{1,0:T(8,128)(2,1)S(1)} %get-tuple-element.88), channel_id=1, source_target_pairs={{0,1},{1,2},{2,3},{3,0},{4,5},{5,6},{6,7},{7,4},{8,9},{9,10},{10,1... | collective-permute-start | bytes 1572872 | tf_op jit(solution)/shard_map/ppermute | solution.py:45
  80.4 13.4 %collective-permute-start.15 = (bf16[128,2048]{1,0:T(8,128)(2,1)S(1)}, bf16[128,2048]{1,0:T(8,128)(2,1)S(1)}, u32[]{:S(2)}, u32[]{:S(2)}) collective-permute-start(bf16[128,2048]{1,0:T(8,128)(2,1)S(1)} %shard_map.87), channel_id=1, source_target_pairs={{0,3},{1,0},{2,1},{3,2},{4,7},{5,4},{6,5},{7,6},{8,11},{9,8},{10,9... | collective-permute-start | bytes 1572872 | tf_op jit(solution)/shard_map/ppermute | solution.py:45
  87.1 18.0 %collective-permute-start.17 = (bf16[128,2048]{1,0:T(8,128)(2,1)S(1)}, bf16[128,2048]{1,0:T(8,128)(2,1)S(1)}, u32[]{:S(2)}, u32[]{:S(2)}) collective-permute-start(bf16[128,2048]{1,0:T(8,128)(2,1)S(1)} %get-tuple-element.86), channel_id=1, source_target_pairs={{0,3},{1,0},{2,1},{3,2},{4,7},{5,4},{6,5},{7,6},{8,11},{9,8},{10,9... | collective-permute-start | bytes 1572872 | tf_op jit(solution)/shard_map/ppermute | solution.py:45
  91.0 26.0 %collective-permute-start.14 = (bf16[128,2048]{1,0:T(8,128)(2,1)S(1)}, bf16[128,2048]{1,0:T(8,128)(2,1)S(1)}, u32[]{:S(2)}, u32[]{:S(2)}) collective-permute-start(bf16[128,2048]{1,0:T(8,128)(2,1)S(1)} %get-tuple-element.82), channel_id=1, source_target_pairs={{0,1},{1,2},{2,3},{3,0},{4,5},{5,6},{6,7},{7,4},{8,9},{9,10},{10,1... | collective-permute-start | bytes 1572872 | tf_op jit(solution)/shard_map/ppermute | solution.py:45
  93.6 22.4 %collective-permute-start.19 = (bf16[128,2048]{1,0:T(8,128)(2,1)S(1)}, bf16[128,2048]{1,0:T(8,128)(2,1)S(1)}, u32[]{:S(2)}, u32[]{:S(2)}) collective-permute-start(bf16[128,2048]{1,0:T(8,128)(2,1)S(1)} %add_convert_fusion), channel_id=1, source_target_pairs={{0,1},{1,2},{2,3},{3,0},{4,5},{5,6},{6,7},{7,4},{8,9},{9,10},{10,1... | collective-permute-start | bytes 1572872 | tf_op jit(solution)/shard_map/ppermute | solution.py:45
  93.9 23.1 %collective-permute-start.16 = (bf16[128,2048]{1,0:T(8,128)(2,1)S(1)}, bf16[128,2048]{1,0:T(8,128)(2,1)S(1)}, u32[]{:S(2)}, u32[]{:S(2)}) collective-permute-start(bf16[128,2048]{1,0:T(8,128)(2,1)S(1)} %add_convert_fusion.1), channel_id=1, source_target_pairs={{0,3},{1,0},{2,1},{3,2},{4,7},{5,4},{6,5},{7,6},{8,11},{9,8},{10,9... | collective-permute-start | bytes 1572872 | tf_op jit(solution)/shard_map/ppermute | solution.py:45

commit v4 on v3

v4 whole, which is shorter than its diff:
```python
import functools

import jax
import jax.numpy as jnp
from jax import lax
from jax.experimental import pallas as pl
from jax.experimental.pallas import tpu as pltpu
from jax.sharding import PartitionSpec as P

HD = 128
TN = 256
MIB = 1 << 20


f32 = jnp.float32
bf16 = jnp.bfloat16
HBM = pl.BlockSpec(memory_space=pltpu.HBM)
VM = pl.BlockSpec(memory_space=pltpu.VMEM)


def ring(n, d):
    return [(i, (i + d) % n) for i in range(n)]


def chip(y, x, c):
    return (y * 4 + x) * 2 + c


def turn(k, first):
    found = []
    for y in range(4):
        for x in range(4):
            for c in range(2):
                along_y = (c == 0) == first
                to = ((y + k) % 4, x, c) if along_y else (y, (x + k) % 4, c)
                found.append((chip(y, x, c), chip(*to)))
    return found


SWAP = [(s, s ^ 1) for s in range(32)]


def shift(v, pairs, axis="tp"):
    return lax.ppermute(v, axis, pairs)


def in_hbm(*arrays):
    return [pltpu.with_memory_space_constraint(v, pltpu.HBM) for v in arrays]


def dot(a, b):
    return jnp.dot(a, b, preferred_element_type=f32)


def params(limit, **more):
    return pltpu.CompilerParams(vmem_limit_bytes=limit * MIB, **more)


def cost(flops, nbytes):
    return pl.CostEstimate(flops=flops, bytes_accessed=nbytes, transcendentals=0)


OWN, LEFT, RIGHT, FAR, CORE0 = range(5)
SCALARS = pl.BlockSpec(memory_space=pltpu.SMEM)


def project_kernel(count, have, riders, info, *refs):
    xs, refs = refs[:count], refs[count:]
    ws, refs = refs[: 3 * count], refs[3 * count :]
    accs, refs = (refs[:3], refs[3:]) if have else (None, refs)
    wide, refs = refs[: len(riders)], refs[len(riders) :]
    outs, refs = refs[:3], refs[3:]
    step = pl.program_id(0)
    copies = []
    for n, (place, col) in enumerate(riders):
        rows, columns = refs[n].shape
        begin = 0 if place is None else pl.multiple_of(info[place] * rows, rows)
        source = wide[n].at[pl.ds(begin, rows), pl.ds(col, columns)]
        copies.append(pltpu.make_async_copy(source, refs[n], refs[-1].at[n]))

    @pl.when(step == 0)
    def _():
        for c in copies:
            c.start()

    cols = pl.ds(pl.multiple_of(step * TN, TN), TN)
    for i in range(3):
        total = accs[i][:, cols] if have else None
        for j in range(count):
            term = dot(xs[j][...], ws[3 * j + i][...])
            total = term if total is None else total + term
        outs[i][:, cols] = total

    @pl.when(step == pl.num_programs(0) - 1)
    def _():
        for c in copies:
            c.wait()


def project(info, pieces, blocks, weights, accs, riders=()):
    count, have = len(pieces), accs is not None
    tok, depth = pieces[0].shape
    width = weights[0].shape[1]

    def wspec(j):
        device, half = blocks[j]
        return pl.BlockSpec((depth, TN), lambda n, i: (2 * i[device] + half, n))

    plan = [(place, col) for _, place, col, _ in riders]
    found = pl.pallas_call(
        functools.partial(project_kernel, count, have, plan),
        out_shape=[pltpu.VMEM((tok, width), f32)] * 3
        + [pltpu.VMEM(shape, bf16) for _, _, _, shape in riders],
        grid_spec=pltpu.PrefetchScalarGridSpec(
            num_scalar_prefetch=1,
            grid=(width // TN,),
            in_specs=[VM] * count
            + [wspec(j) for j in range(count) for _ in range(3)]
            + ([VM] * 3 if have else [])
            + [HBM] * len(riders),
            out_specs=[VM] * (3 + len(riders)),
            scratch_shapes=[pltpu.SemaphoreType.DMA((max(len(riders), 1),))],
        ),
        compiler_params=params(16),
        cost_estimate=cost(6 * count * tok * depth * width, 6 * count * depth * width),
    )(info, *pieces, *(list(weights) * count), *(accs or ()), *(w for w, _, _, _ in riders))
    return found[:3], found[3:]


def split_kernel(codes, a, b, sem):
    half = a.shape[1]
    copies = [
        pltpu.make_async_copy(codes.at[:, pl.ds(0, half)], a, sem.at[0]),
        pltpu.make_async_copy(codes.at[:, pl.ds(half, half)], b, sem.at[1]),
    ]
    for c in copies:
        c.start()
    for c in copies:
        c.wait()


def split(codes):
    tok, part = codes.shape
    return pl.pallas_call(
        split_kernel,
        out_shape=[pltpu.VMEM((tok, part // 2), bf16)] * 2,
        in_specs=[HBM],
        out_specs=[VM] * 2,
        scratch_shapes=[pltpu.SemaphoreType.DMA((2,))],
        compiler_params=params(4),
        cost_estimate=cost(0, 2 * MIB),
    )(codes)


def feature(t):
    return jnp.where(t > 0, t + 1.0, jnp.exp(t)).astype(bf16)


def last_terms(xa, xb, w, acc, scale, rows, cols):
    half = xa.shape[1]
    t = acc[rows, cols] + dot(xa[...], w[pl.ds(0, half), cols])
    return (t + dot(xb[...], w[pl.ds(half, half), cols])) * scale[rows, :]


def own_state(k, v):
    return lax.dot_general(k, v, (((0,), (0,)), ((), ())), preferred_element_type=f32)


def early_kv_kernel(xa, xb, wk, wv, acck, accv, scale, wide, fk, vb, state, near, sem):
    copy = pltpu.make_async_copy(wide.at[:, pl.ds(0, near.shape[1])], near, sem)
    copy.start()
    rows = slice(0, fk.shape[0])
    for n in range(fk.shape[1] // TN):
        cols = slice(n * TN, (n + 1) * TN)
        k = feature(last_terms(xa, xb, wk, acck, scale, rows, cols))
        v = last_terms(xa, xb, wv, accv, scale, rows, cols).astype(bf16)
        fk[:, cols] = k
        vb[:, cols] = v
        for h in range(TN // HD):
            cut = slice(h * HD, (h + 1) * HD)
            state[n * (TN // HD) + h] = own_state(k[:, cut], v[:, cut])
    copy.wait()


def early_kv(xa, xb, wk, wv, acck, accv, scale, w_out):
    tok, width = xa.shape[0], acck.shape[1]
    return pl.pallas_call(
        early_kv_kernel,
        out_shape=[
            pltpu.VMEM((tok, width), bf16),
            pltpu.VMEM((tok, width), bf16),
            pltpu.VMEM((width // HD, HD, HD), f32),
            pltpu.VMEM((w_out.shape[0], w_out.shape[1] // 2), bf16),
        ],
        in_specs=[VM] * 7 + [HBM],
        out_specs=[VM] * 4,
        scratch_shapes=[pltpu.SemaphoreType.DMA],
        compiler_params=params(12),
        cost_estimate=cost(4 * tok * 1024 * width, 4 * MIB),
    )(xa, xb, wk, wv, acck, accv, scale, w_out)


def late_kv_kernel(part, info, xa, xb, wk, wv, acck, accv, scale, early, fk, vb, state):
    tok, width = fk.shape
    core = 1 - info[CORE0]
    place = core if part == 0 else 1 - core
    rows = slice(tok, 2 * tok)
    for n in range(width // TN):
        cols = pl.ds(pl.multiple_of(place * width + n * TN, TN), TN)
        ocols = slice(n * TN, (n + 1) * TN)
        k = feature(last_terms(xa, xb, wk, acck, scale, rows, cols))
        v = last_terms(xa, xb, wv, accv, scale, rows, cols).astype(bf16)
        fk[:, ocols] = k
        vb[:, ocols] = v
        for h in range(TN // HD):
            cut = slice(h * HD, (h + 1) * HD)
            at = n * (TN // HD) + h
            total = early[place * (width // HD) + at] + own_state(k[:, cut], v[:, cut])
            state[at] = total.astype(state.dtype)


def late_kv(part, info, xa, xb, wk, wv, acck, accv, scale, early):
    tok, width = xa.shape[0], acck.shape[1] // 2
    return pl.pallas_call(
        functools.partial(late_kv_kernel, part),
        out_shape=[
            pltpu.VMEM((tok, width), bf16),
            pltpu.VMEM((tok, width), bf16),
            pltpu.VMEM((width // HD, HD, HD), f32 if part == 0 else bf16),
        ],
        in_specs=[SCALARS] + [VM] * 8,
        out_specs=[VM] * 3,
        compiler_params=params(12),
        cost_estimate=cost(4 * tok * 1024 * width, 4 * MIB),
    )(info, xa, xb, wk, wv, acck, accv, scale, early)


def last_q_kernel(xa1, xa2, xb1, xb2, w, acc, scale, fq):
    tok = xa1.shape[0]
    for n in range(fq.shape[1] // TN):
        cols = slice(n * TN, (n + 1) * TN)
        for i, (xa, xb) in enumerate(((xa1, xb1), (xa2, xb2))):
            rows = slice(i * tok, (i + 1) * tok)
            fq[rows, cols] = feature(last_terms(xa, xb, w, acc, scale, rows, cols))


def last_q(xa, xb, w, acc, scale):
    tok, width = acc.shape
    return pl.pallas_call(
        last_q_kernel,
        out_shape=pltpu.VMEM((tok, width), bf16),
        in_specs=[VM] * 7,
        out_specs=VM,
        compiler_params=params(12),
        cost_estimate=cost(2 * tok * 1024 * width, 4 * MIB),
    )(*xa, *xb, w, acc, scale)


def within_kernel(part, info, fq, k_early, v_early, k_late, v_late, out):
    rows, width = k_late.shape
    row = lax.broadcasted_iota(jnp.int32, (rows, rows), 0)
    col = lax.broadcasted_iota(jnp.int32, (rows, rows), 1)
    keep = row >= col
    core = 1 - info[CORE0]
    start = (core if part == 0 else 1 - core) * width

    def scores(q, k):
        return lax.dot_general(q, k, (((1,), (1,)), ((), ())), preferred_element_type=f32)

    def masked(q, k):
        return jnp.where(keep, scores(q, k), 0.0).astype(bf16)

    for h in range(width // HD):
        qcols = pl.ds(pl.multiple_of(start + h * HD, HD), HD)
        cols = slice(h * HD, (h + 1) * HD)
        k, v = k_early[:, qcols], v_early[:, qcols]
        q = fq[0:rows, qcols]
        out[0:rows, cols] = dot(masked(q, k), v)
        q = fq[rows : 2 * rows, qcols]
        y = dot(scores(q, k).astype(bf16), v)
        out[rows : 2 * rows, cols] = y + dot(masked(q, k_late[:, cols]), v_late[:, cols])


def within(part, info, fq, *keys):
    tok, width = fq.shape[0], fq.shape[1] // 2
    return pl.pallas_call(
        functools.partial(within_kernel, part),
        out_shape=pltpu.VMEM((tok, width), f32),
        in_specs=[SCALARS] + [VM] * 5,
        out_specs=VM,
        compiler_params=params(12),
        cost_estimate=cost(4 * width * tok * tok, 4 * MIB),
    )(info, fq, *keys)


def normed(info, place, fq, ys, states, gain, o):
    rows, width = o.shape
    mine = pl.ds(pl.multiple_of(info[place] * rows, rows), rows)
    core = 1 - info[CORE0]
    for part in range(2):
        start = (core if part == 0 else 1 - core) * (width // 2)
        for g in range(width // HD // 2):
            cols = pl.ds(pl.multiple_of(start + g * HD, HD), HD)
            y = ys[part][mine, g * HD : (g + 1) * HD] + dot(fq[mine, cols], states[part][g])
            ms = jnp.mean(y * y, axis=-1, keepdims=True)
            o[:, cols] = (y * lax.rsqrt(ms + 1e-05) * gain[:, cols]).astype(bf16)


def project_out(o, wos, outs):
    for wo, out in zip(wos, outs):

        @pl.loop(0, out.shape[1] // 512)
        def _(n):
            cols = pl.ds(pl.multiple_of(n * 512, 512), 512)
            out[:, cols] = dot(o[...], wo[:, cols]).astype(out.dtype)


def first_kernel(place, sides, info, fq, y0, y1, own, back, gain, *refs):
    normed(info, place, fq, (y0, y1), (own, back), gain, refs[sides])
    project_out(refs[sides], refs[:sides], refs[sides + 1 :])


def first_share(info, place, wos, types, fq, y0, y1, own, back, gain):
    tok, width = fq.shape
    rows, half = tok // 4, wos[0].shape[1]
    return pl.pallas_call(
        functools.partial(first_kernel, place, len(wos)),
        out_shape=[pltpu.VMEM((rows, width), bf16)] + [pltpu.VMEM((rows, half), t) for t in types],
        in_specs=[SCALARS] + [VM] * (6 + len(wos)),
        out_specs=[VM] * (1 + len(wos)),
        compiler_params=params(12),
        cost_estimate=cost(2 * rows * width * half * len(wos), 4 * MIB),
    )(info, fq, y0, y1, own, back, gain, *wos)


def more_kernel(o, wo, out):
    project_out(o, (wo,), (out,))


def more_share(o, wo):
    rows, half = o.shape[0], wo.shape[1]
    return pl.pallas_call(
        more_kernel,
        out_shape=pltpu.VMEM((rows, half), bf16),
        in_specs=[VM] * 2,
        out_specs=VM,
        compiler_params=params(12),
        cost_estimate=cost(2 * rows * o.shape[1] * half, 4 * MIB),
    )(o, wo)


def finish_kernel(side, own, one, two, *refs):
    out, total, sem = refs[-3:]
    half = own.shape[1]
    sums = own[...] + one[...].astype(f32) + two[...].astype(f32)
    total[...] = sums.astype(bf16)
    copy = pltpu.make_async_copy(total, out.at[:, pl.ds(side * half, half)], sem)
    copy.start()
    copy.wait()


def finish(side, own, one, two, out):
    rows, half = own.shape
    given = () if out is None else (out,)
    return pl.pallas_call(
        functools.partial(finish_kernel, side),
        out_shape=pltpu.HBM((rows, 2 * half), bf16),
        in_specs=[VM] * 3 + [HBM] * len(given),
        out_specs=HBM,
        input_output_aliases={3: 0} if given else {},
        scratch_shapes=[pltpu.VMEM((rows, half), bf16), pltpu.SemaphoreType.DMA],
        compiler_params=params(8),
        cost_estimate=cost(rows * half, 3 * MIB),
    )(own, one, two, *given)


def before_this(flags, mine, other):
    core0, core1, seen_a, later_b, seen_b = flags[0], flags[1], flags[2:5], flags[5:8], flags[8:]

    def send(v, pairs):
        return shift(v.astype(bf16), pairs, "seq").astype(f32)

    theirs = send(other, SWAP)
    both = mine + theirs
    r = {k: send(both, turn(k, True)) for k in (2, 1, 3)}
    earlier = seen_a[0] * r[1] + seen_a[1] * r[2] + seen_a[2] * r[3]
    total = core0 * earlier + core1 * (both + r[1] + r[2] + r[3])
    t = {k: send(total + later_b[k - 1] * both, turn(k, False)) for k in (2, 1, 3)}
    prefix = earlier + seen_b[0] * t[1] + seen_b[1] * t[2] + seen_b[2] * t[3]
    own = (prefix + core1 * theirs).astype(bf16)
    return own, send(prefix + core0 * mine, SWAP).astype(bf16)


def on_device(codes, exponents, w_query, w_key, w_value, norm_gain, w_out):
    z = lax.axis_index("tp")
    s = lax.axis_index("seq")
    core, x, y = s % 2, (s // 2) % 4, s // 8
    first, second = jnp.where(core == 0, y, x), jnp.where(core == 0, x, y)
    info = jnp.stack([z, (z + 3) % 4, (z + 1) % 4, (z + 2) % 4, 1 - core]).astype(jnp.int32)
    core0, core1 = core == 0, core == 1
    flags = [core0, core1]
    flags += [first >= k for k in (1, 2, 3)]
    flags += [core0 & (second < 4 - k) for k in (1, 2, 3)]
    flags += [core0 | (second >= k) for k in (1, 2, 3)]
    flags = [v.astype(f32) for v in flags]
    tok, part = codes.shape
    width = w_query.shape[1]
    half = w_out.shape[1] // 2
    scale = jnp.exp2(exponents.astype(f32))[:, None]
    gain = norm_gain.reshape(1, width)
    codes, info, *flags = lax.optimization_barrier((codes, info, *flags))
    up, down = ring(4, 1), ring(4, -1)
    weights, w_out = in_hbm(w_query, w_key, w_value), in_hbm(w_out)[0]

    a, b = split(in_hbm(codes)[0])
    a_left = shift(a, up)
    b_right = shift(b, down)
    b_left = shift(b, up)
    a_right = shift(a, down)
    early = tok // 2
    a_far1 = shift(a_left[:early], up)
    b_far1 = shift(b_right[:early], down)
    a_far2 = shift(a_left[early:], up)
    b_far2 = shift(b_right[early:], down)

    accs, (wk_far, wv_far, wq_far) = project(
        info,
        (a, b),
        ((OWN, 0), (OWN, 1)),
        weights,
        None,
        [(weights[n], FAR, 0, (part, width)) for n in (1, 2, 0)],
    )
    accs, (wo_l,) = project(
        info,
        (a_left, b_right),
        ((LEFT, 0), (RIGHT, 1)),
        weights,
        accs,
        [(w_out, None, half, (w_out.shape[0], half))],
    )
    accs, _ = project(info, (b_left, a_right), ((LEFT, 1), (RIGHT, 0)), weights, accs)
    last = (wk_far, wv_far, accs[1], accs[2], scale)
    k_early, v_early, state, wo_u = early_kv(a_far1, b_far1, *last, w_out)
    k1, v1, other = late_kv(1, info, a_far2, b_far2, *last, state)
    k0, v0, mine = late_kv(0, info, a_far2, b_far2, *last, state)
    own, back = before_this(flags, mine, other)
    feat_q = last_q((a_far1, a_far2), (b_far1, b_far2), wq_far, accs[0], scale)
    y0 = within(0, info, feat_q, k_early, v_early, k0, v0)
    y1 = within(1, info, feat_q, k_early, v_early, k1, v1)

    rest = (feat_q, y0, y1, own, back, gain)
    o, u_far = first_share(info, FAR, (wo_u,), (bf16,), *rest)
    u_pass = shift(u_far, up)
    l_pass = shift(more_share(o, wo_l), down)
    _, l_next, u_next = first_share(info, RIGHT, (wo_l, wo_u), (bf16, f32), *rest)
    l_low = shift(l_next, up)
    _, u_prev, l_prev = first_share(info, LEFT, (wo_u, wo_l), (bf16, f32), *rest)
    u_high = shift(u_prev, down)
    _, u, l = first_share(info, OWN, (wo_u, wo_l), (f32, f32), *rest)
    u_low = shift((u_next + u_pass.astype(f32)).astype(bf16), up)
    l_high = shift((l_prev + l_pass.astype(f32)).astype(bf16), down)
    out = finish(0, u, u_high, u_low, None)
    return finish(1, l, l_low, l_high, out)


def solution(mesh):
    in_specs = (
        P("seq", "tp"),
        P("seq"),
        P(None, "tp"),
        P(None, "tp"),
        P(None, "tp"),
        P("tp"),
        P("tp", None),
    )
    out_specs = P(("seq", "tp"), None)

    return jax.shard_map(
        on_device, mesh=mesh, in_specs=in_specs, out_specs=out_specs, check_vma=False
    )
```

time: 119 us -> 130 us (1.092)
  waiting for transfers between devices: 28.6 us -> 39 us
  Pallas kernels: 55.9 us -> 52.2 us
  starting transfers between devices: 31.6 us -> 35.3 us
    ppermute x20 -> x22, waiting for transfers between devices: 28.6 us -> 39 us  [shift(): return lax.ppermute(v, axis, pairs)]
    ppermute x20 -> x22, starting transfers between devices: 31.6 us -> 35.3 us  [shift(): return lax.ppermute(v, axis, pairs)]
    pallas_call x11, Pallas kernels: 45.3 us -> 43 us  [the longest x3 21.9 us: project(): pl.pallas_call(functools.partial(project_kernel, count, have, plan), out_...]
  transfers between devices with their start and end apart: 20 -> 22, of which waited for: 9 -> 9; matrix products, arithmetic and copies ran while one was open for 1% -> 1% of each run, Pallas kernels for 42% -> 36%
where the time goes in v4:
time: 130 us; the launch traced here: 129 us
  Pallas kernels  52.2 us (40%)
  waiting for transfers between devices  39 us (30%)
  starting transfers between devices  35.3 us (27%)
  other arithmetic  1.41 us (1%)
    ppermute x22, waiting for transfers between devices, shift(): return lax.ppermute(v, axis, pairs)  39 us
    ppermute x22, starting transfers between devices, shift(): return lax.ppermute(v, axis, pairs)  35.3 us
    pallas_call x3, Pallas kernels, project(): pl.pallas_call(functools.partial(project_kernel, count, have, plan), out_...  21.9 us
    pallas_call x4, Pallas kernels, first_share(): pl.pallas_call(functools.partial(first_kernel, place, len(wos)), out_shap...  13.9 us
    pallas_call x2, Pallas kernels, within(): pl.pallas_call(functools.partial(within_kernel, part), out_shape=pltpu.VM...  4.47 us
    pallas_call x2, Pallas kernels, late_kv(): pl.pallas_call(functools.partial(late_kv_kernel, part), out_shape=[pltpu....  3.52 us
  transfers between devices with their start and end apart: 22, of which 9 were waited for; matrix products, arithmetic and copies ran while one was open for 1% of the time, Pallas kernels for 36%

profile of v4, /device:TPU:1, one launch (start us, length us, event | category | flops | bytes accessed | tf_op | source)
XLA Modules:
  0.0 128.7 jit_solution(4325879822441058079)
XLA Ops:
  1.3 4.6 %collective-permute-start.3 = (bf16[512,512]{1,0:T(8,128)(2,1)S(1)}, bf16[512,512]{1,0:T(8,128)(2,1)S(1)}, u32[]{:S(2)}, u32[]{:S(2)}) collective-permute-start(bf16[512,512]{1,0:T(8,128)(2,1)S(1)} %get-tuple-element.54.refs_1_), channel_id=1, source_target_pairs={{0,3},{1,0},{2,1},{3,2},{4,7},{5,4},{6,5},{7,6},{8,11},{9,8},{10,9... | collective-permute-start | bytes 1572872 | tf_op jit(solution)/shard_map/ppermute | solution.py:44
  6.0 2.7 %collective-permute-start.7 = (bf16[512,512]{1,0:T(8,128)(2,1)S(1)}, bf16[512,512]{1,0:T(8,128)(2,1)S(1)}, u32[]{:S(2)}, u32[]{:S(2)}) collective-permute-start(bf16[512,512]{1,0:T(8,128)(2,1)S(1)} %get-tuple-element.53.refs_0_), channel_id=1, source_target_pairs={{0,3},{1,0},{2,1},{3,2},{4,7},{5,4},{6,5},{7,6},{8,11},{9,8},{10,9... | collective-permute-start | bytes 1572872 | tf_op jit(solution)/shard_map/ppermute | solution.py:44
  9.5 8.0 %shard_map.74 = (f32[512,1024]{1,0:T(8,128)S(1)}, f32[512,1024]{1,0:T(8,128)S(1)}, f32[512,1024]{1,0:T(8,128)S(1)}, bf16[1024,1024]{1,0:T(8,128)(2,1)S(1)}, bf16...) custom-call(s32[5]{0:T(128)S(1)} %stack.23.info, bf16[512,512]{1,0:T(8,128)(2,1)S(1)} %get-tuple-element.53.refs_0_, ...), custom_call_target="tpu_custom_call" | custom-call | flops 3221225472 | bytes 6291456 | tf_op jit(solution)/shard_map/pallas_call | solution.py:110
  17.5 13.4 %collective-permute-done.refs_0_ = bf16[512,512]{1,0:T(8,128)(2,1)S(1)} collective-permute-done((bf16[512,512]{1,0:T(8,128)(2,1)S(1)}, bf16[512,512]{1,0:T(8,128)(2,1)S(1)}, u32[]{:S(2)}, u32[]{:S(2)}) %collective-permute-start) | collective-permute-done | bytes 524320 | tf_op jit(solution)/shard_map/ppermute | solution.py:44
  31.1 2.7 %collective-permute-start.4 = (bf16[256,512]{1,0:T(8,128)(2,1)S(1)}, bf16[256,512]{1,0:T(8,128)(2,1)S(1)}, u32[]{:S(2)}, u32[]{:S(2)}) collective-permute-start(bf16[256,512]{1,0:T(8,128)(2,1)S(1)} %get-tuple-element.103), channel_id=1, source_target_pairs={{0,3},{1,0},{2,1},{3,2},{4,7},{5,4},{6,5},{7,6},{8,11},{9,8},{10,9... | collective-permute-start | bytes 786440 | tf_op jit(solution)/shard_map/ppermute | solution.py:44
  33.8 7.4 %shard_map.75 = (f32[512,1024]{1,0:T(8,128)S(1)}, f32[512,1024]{1,0:T(8,128)S(1)}, f32[512,1024]{1,0:T(8,128)S(1)}, bf16[1024,2048]{1,0:T(8,128)(2,1)S(1)}) custom-call(s32[5]{0:T(128)S(1)} %stack.23.info, bf16[512,512]{1,0:T(8,128)(2,1)S(1)} %collective-permute-done.refs_0_, bf16[512,512]{1,0:T(8,128)(2,1)S(1)} %collective-permute-done.3.refs_1_, ...), custom_call_target="tpu_custom_call" | custom-call | flops 3221225472 | bytes 6291456 | tf_op jit(solution)/shard_map/pallas_call | solution.py:110
  41.3 2.7 %collective-permute-start.5 = (bf16[256,512]{1,0:T(8,128)(2,1)S(1)}, bf16[256,512]{1,0:T(8,128)(2,1)S(1)}, u32[]{:S(2)}, u32[]{:S(2)}) collective-permute-start(bf16[256,512]{1,0:T(8,128)(2,1)S(1)} %get-tuple-element.102), channel_id=1, source_target_pairs={{0,3},{1,0},{2,1},{3,2},{4,7},{5,4},{6,5},{7,6},{8,11},{9,8},{10,9... | collective-permute-start | bytes 786440 | tf_op jit(solution)/shard_map/ppermute | solution.py:44
  44.0 6.5 %shard_map.76 = (f32[512,1024]{1,0:T(8,128)S(1)}, f32[512,1024]{1,0:T(8,128)S(1)}, f32[512,1024]{1,0:T(8,128)S(1)}) custom-call(s32[5]{0:T(128)S(1)} %stack.23.info, bf16[512,512]{1,0:T(8,128)(2,1)S(1)} %collective-permute-done.6.refs_0_, bf16[512,512]{1,0:T(8,128)(2,1)S(1)} %collective-permute-done.7.refs_1_, bf16[4096,1024]{1,0:T(8,128)(2,1)} %refs_5_.5, ...), custom_call_target="tpu_custom_call" | custom-call | flops 3221225472 | bytes 6291456 | tf_op jit(solution)/shard_map/pallas_call | solution.py:110
  50.6 2.3 %shard_map.78 = (bf16[256,1024]{1,0:T(8,128)(2,1)S(1)}, bf16[256,1024]{1,0:T(8,128)(2,1)S(1)}, f32[8,128,128]{2,1,0:T(8,128)S(1)}, bf16[1024,2048]{1,0:T(8,128)(2,1)S(1)}) custom-call(bf16[256,512]{1,0:T(8,128)(2,1)S(1)} %collective-permute-done.1.xa1.xa, bf16[256,512]{1,0:T(8,128)(2,1)S(1)} %collective-permute-done.4.xb1.xb, ...), custom_call_target="tpu_custom_call" | custom-call | flops 1073741824 | bytes 4194304 | tf_op jit(solution)/shard_map/pallas_call | solution.py:187
  54.7 3.0 %collective-permute-start.8 = (bf16[4,128,128]{2,1,0:T(8,128)(2,1)S(1)}, bf16[4,128,128]{2,1,0:T(8,128)(2,1)S(1)}, u32[]{:S(2)}, u32[]{:S(2)}) collective-permute-start(bf16[4,128,128]{2,1,0:T(8,128)(2,1)S(1)} %get-tuple-element.76), channel_id=1, source_target_pairs={{0,4},{4,0},{8,12},{12,8},{16,20},{20,16},{24,28},{28,24},{32,36},... | collective-permute-start | bytes 393224 | tf_op jit(solution)/shard_map/ppermute | solution.py:44
  59.5 2.8 %collective-permute-start.10 = (bf16[4,128,128]{2,1,0:T(8,128)(2,1)S(1)}, bf16[4,128,128]{2,1,0:T(8,128)(2,1)S(1)}, u32[]{:S(2)}, u32[]{:S(2)}) collective-permute-start(bf16[4,128,128]{2,1,0:T(8,128)(2,1)S(1)} %fusion.6), channel_id=1, source_target_pairs={{0,64},{4,20},{8,72},{12,28},{16,80},{20,4},{24,88},{28,12},{32,96... | collective-permute-start | bytes 393224 | tf_op jit(solution)/shard_map/ppermute | solution.py:44
  66.7 1.8 %collective-permute-done.9 = bf16[4,128,128]{2,1,0:T(8,128)(2,1)S(1)} collective-permute-done((bf16[4,128,128]{2,1,0:T(8,128)(2,1)S(1)}, bf16[4,128,128]{2,1,0:T(8,128)(2,1)S(1)}, u32[]{:S(2)}, u32[]{:S(2)}) %collective-permute-start.9) | collective-permute-done | bytes 131104 | tf_op jit(solution)/shard_map/ppermute | solution.py:44
  69.8 2.6 %collective-permute-start.13 = (bf16[4,128,128]{2,1,0:T(8,128)(2,1)S(1)}, bf16[4,128,128]{2,1,0:T(8,128)(2,1)S(1)}, u32[]{:S(2)}, u32[]{:S(2)}) collective-permute-start(bf16[4,128,128]{2,1,0:T(8,128)(2,1)S(1)} %get-tuple-element.100), channel_id=1, source_target_pairs={{0,16},{4,68},{8,24},{12,76},{16,0},{20,84},{24,8},{28,92},{32,48}... | collective-permute-start | bytes 393224 | tf_op jit(solution)/shard_map/ppermute | solution.py:44
  75.1 2.2 %shard_map.82.y1 = f32[512,512]{1,0:T(8,128)S(1)} custom-call(s32[5]{0:T(128)S(1)} %stack.23.info, bf16[512,1024]{1,0:T(8,128)(2,1)S(1)} %shard_map.77.fq, bf16[256,1024]{1,0:T(8,128)(2,1)S(1)} %get-tuple-element.67.k_early, bf16[256,1024]{1,0:T(8,128)(2,1)S(1)} %get-tuple-element.68.v_early, bf16[256,512]{1,0:T(8,128)(2,1)S(1)} %get-tuple-element.72.k_late, ...), custom_call_target="tpu_custom_call" | custom-call | flops 536870912 | bytes 4194304 | tf_op jit(solution)/shard_map/pallas_call | solution.py:286
  77.4 2.2 %shard_map.80.y0 = f32[512,512]{1,0:T(8,128)S(1)} custom-call(s32[5]{0:T(128)S(1)} %stack.23.info, bf16[512,1024]{1,0:T(8,128)(2,1)S(1)} %shard_map.77.fq, bf16[256,1024]{1,0:T(8,128)(2,1)S(1)} %get-tuple-element.67.k_early, bf16[256,1024]{1,0:T(8,128)(2,1)S(1)} %get-tuple-element.68.v_early, bf16[256,512]{1,0:T(8,128)(2,1)S(1)} %get-tuple-element.70.k_late, ...), custom_call_target="tpu_custom_call" | custom-call | flops 536870912 | bytes 4194304 | tf_op jit(solution)/shard_map/pallas_call | solution.py:286
  79.8 2.6 %collective-permute-start.15 = (bf16[4,128,128]{2,1,0:T(8,128)(2,1)S(1)}, bf16[4,128,128]{2,1,0:T(8,128)(2,1)S(1)}, u32[]{:S(2)}, u32[]{:S(2)}) collective-permute-start(bf16[4,128,128]{2,1,0:T(8,128)(2,1)S(1)} %get-tuple-element.97), channel_id=1, source_target_pairs={{0,4},{4,0},{8,12},{12,8},{16,20},{20,16},{24,28},{28,24},{32,36},... | collective-permute-start | bytes 393224 | tf_op jit(solution)/shard_map/ppermute | solution.py:44
  83.4 2.2 %shard_map.86 = (bf16[128,1024]{1,0:T(8,128)(2,1)S(1)}, bf16[128,2048]{1,0:T(8,128)(2,1)S(1)}) custom-call(s32[5]{0:T(128)S(1)} %stack.23.info, bf16[512,1024]{1,0:T(8,128)(2,1)S(1)} %shard_map.77.fq, f32[512,512]{1,0:T(8,128)S(1)} %shard_map.80.y0, f32[512,512]{1,0:T(8,128)S(1)} %shard_map.82.y1, bf16[4,128,128]{2,1,0:T(8,128)(2,1)S(1)} %fusion.1.own, ...), custom_call_target="tpu_custom_call" | custom-call | flops 536870912 | bytes 4194304 | tf_op jit(solution)/shard_map/pallas_call | solution.py:326
  85.7 3.9 %shard_map.85 = (bf16[128,1024]{1,0:T(8,128)(2,1)}, bf16[128,2048]{1,0:T(8,128)(2,1)S(1)}, f32[128,2048]{1,0:T(8,128)S(1)}) custom-call(s32[5]{0:T(128)S(1)} %stack.23.info, bf16[512,1024]{1,0:T(8,128)(2,1)S(1)} %shard_map.77.fq, f32[512,512]{1,0:T(8,128)S(1)} %shard_map.80.y0, f32[512,512]{1,0:T(8,128)S(1)} %shard_map.82.y1, ...), custom_call_target="tpu_custom_call" | custom-call | flops 1073741824 | bytes 4194304 | tf_op jit(solution)/shard_map/pallas_call | solution.py:326
  89.6 2.7 %collective-permute-start.19 = (bf16[128,2048]{1,0:T(8,128)(2,1)S(1)}, bf16[128,2048]{1,0:T(8,128)(2,1)S(1)}, u32[]{:S(2)}, u32[]{:S(2)}) collective-permute-start(bf16[128,2048]{1,0:T(8,128)(2,1)S(1)} %get-tuple-element.94), channel_id=1, source_target_pairs={{0,3},{1,0},{2,1},{3,2},{4,7},{5,4},{6,5},{7,6},{8,11},{9,8},{10,9... | collective-permute-start | bytes 1572872 | tf_op jit(solution)/shard_map/ppermute | solution.py:44
  93.6 3.9 %shard_map.84 = (bf16[128,1024]{1,0:T(8,128)(2,1)}, bf16[128,2048]{1,0:T(8,128)(2,1)S(1)}, f32[128,2048]{1,0:T(8,128)S(1)}) custom-call(s32[5]{0:T(128)S(1)} %stack.23.info, bf16[512,1024]{1,0:T(8,128)(2,1)S(1)} %shard_map.77.fq, f32[512,512]{1,0:T(8,128)S(1)} %shard_map.80.y0, f32[512,512]{1,0:T(8,128)S(1)} %shard_map.82.y1, ...), custom_call_target="tpu_custom_call" | custom-call | flops 1073741824 | bytes 4194304 | tf_op jit(solution)/shard_map/pallas_call | solution.py:326
  100.2 13.9 %collective-permute-done.17 = bf16[128,2048]{1,0:T(8,128)(2,1)S(1)} collective-permute-done((bf16[128,2048]{1,0:T(8,128)(2,1)S(1)}, bf16[128,2048]{1,0:T(8,128)(2,1)S(1)}, u32[]{:S(2)}, u32[]{:S(2)}) %collective-permute-start.17) | collective-permute-done | bytes 524320 | tf_op jit(solution)/shard_map/ppermute | solution.py:44
  114.3 3.5 %collective-permute-start.18 = (bf16[128,2048]{1,0:T(8,128)(2,1)S(1)}, bf16[128,2048]{1,0:T(8,128)(2,1)S(1)}, u32[]{:S(2)}, u32[]{:S(2)}) collective-permute-start(bf16[128,2048]{1,0:T(8,128)(2,1)S(1)} %add_convert_fusion.1), channel_id=1, source_target_pairs={{0,3},{1,0},{2,1},{3,2},{4,7},{5,4},{6,5},{7,6},{8,11},{9,8},{10,9... | collective-permute-start | bytes 1572872 | tf_op jit(solution)/shard_map/ppermute | solution.py:44
  117.8 3.9 %shard_map.83 = (bf16[128,1024]{1,0:T(8,128)(2,1)}, f32[128,2048]{1,0:T(8,128)S(1)}, f32[128,2048]{1,0:T(8,128)S(1)}) custom-call(s32[5]{0:T(128)S(1)} %stack.23.info, bf16[512,1024]{1,0:T(8,128)(2,1)S(1)} %shard_map.77.fq, f32[512,512]{1,0:T(8,128)S(1)} %shard_map.80.y0, f32[512,512]{1,0:T(8,128)S(1)} %shard_map.82.y1, bf16[4,128,128]{2,1,0:T(8,128)(2,1)S(1)} %fusion.1.own, ...), custom_call_target="tpu_custom_call" | custom-call | flops 1073741824 | bytes 4194304 | tf_op jit(solution)/shard_map/pallas_call | solution.py:326
  123.6 4.0 %collective-permute-done.18.two = bf16[128,2048]{1,0:T(8,128)(2,1)S(1)} collective-permute-done((bf16[128,2048]{1,0:T(8,128)(2,1)S(1)}, bf16[128,2048]{1,0:T(8,128)(2,1)S(1)}, u32[]{:S(2)}, u32[]{:S(2)}) %collective-permute-start.18) | collective-permute-done | bytes 524320 | tf_op jit(solution)/shard_map/ppermute | solution.py:44
  (50 shorter events, 22.5 us)
Async XLA Ops:
  1.3 29.7 %collective-permute-start.3 = (bf16[512,512]{1,0:T(8,128)(2,1)S(1)}, bf16[512,512]{1,0:T(8,128)(2,1)S(1)}, u32[]{:S(2)}, u32[]{:S(2)}) collective-permute-start(bf16[512,512]{1,0:T(8,128)(2,1)S(1)} %get-tuple-element.54.refs_1_), channel_id=1, source_target_pairs={{0,3},{1,0},{2,1},{3,2},{4,7},{5,4},{6,5},{7,6},{8,11},{9,8},{10,9... | collective-permute-start | bytes 1572872 | tf_op jit(solution)/shard_map/ppermute | solution.py:44
  6.0 35.3 %collective-permute-start.6 = (bf16[512,512]{1,0:T(8,128)(2,1)S(1)}, bf16[512,512]{1,0:T(8,128)(2,1)S(1)}, u32[]{:S(2)}, u32[]{:S(2)}) collective-permute-start(bf16[512,512]{1,0:T(8,128)(2,1)S(1)} %get-tuple-element.54.refs_1_), channel_id=1, source_target_pairs={{0,1},{1,2},{2,3},{3,0},{4,5},{5,6},{6,7},{7,4},{8,9},{9,10},{10,1... | collective-permute-start | bytes 1572872 | tf_op jit(solution)/shard_map/ppermute | solution.py:44
  6.0 25.0 %collective-permute-start = (bf16[512,512]{1,0:T(8,128)(2,1)S(1)}, bf16[512,512]{1,0:T(8,128)(2,1)S(1)}, u32[]{:S(2)}, u32[]{:S(2)}) collective-permute-start(bf16[512,512]{1,0:T(8,128)(2,1)S(1)} %get-tuple-element.53.refs_0_), channel_id=1, source_target_pairs={{0,1},{1,2},{2,3},{3,0},{4,5},{5,6},{6,7},{7,4},{8,9},{9,10},{10,1... | collective-permute-start | bytes 1572872 | tf_op jit(solution)/shard_map/ppermute | solution.py:44
  6.0 38.0 %collective-permute-start.7 = (bf16[512,512]{1,0:T(8,128)(2,1)S(1)}, bf16[512,512]{1,0:T(8,128)(2,1)S(1)}, u32[]{:S(2)}, u32[]{:S(2)}) collective-permute-start(bf16[512,512]{1,0:T(8,128)(2,1)S(1)} %get-tuple-element.53.refs_0_), channel_id=1, source_target_pairs={{0,3},{1,0},{2,1},{3,2},{4,7},{5,4},{6,5},{7,6},{8,11},{9,8},{10,9... | collective-permute-start | bytes 1572872 | tf_op jit(solution)/shard_map/ppermute | solution.py:44
  31.0 19.6 %collective-permute-start.1 = (bf16[256,512]{1,0:T(8,128)(2,1)S(1)}, bf16[256,512]{1,0:T(8,128)(2,1)S(1)}, u32[]{:S(2)}, u32[]{:S(2)}) collective-permute-start(bf16[256,512]{1,0:T(8,128)(2,1)S(1)} %get-tuple-element.105), channel_id=1, source_target_pairs={{0,1},{1,2},{2,3},{3,0},{4,5},{5,6},{6,7},{7,4},{8,9},{9,10},{10,1... | collective-permute-start | bytes 786440 | tf_op jit(solution)/shard_map/ppermute | solution.py:44
  31.1 19.5 %collective-permute-start.4 = (bf16[256,512]{1,0:T(8,128)(2,1)S(1)}, bf16[256,512]{1,0:T(8,128)(2,1)S(1)}, u32[]{:S(2)}, u32[]{:S(2)}) collective-permute-start(bf16[256,512]{1,0:T(8,128)(2,1)S(1)} %get-tuple-element.103), channel_id=1, source_target_pairs={{0,3},{1,0},{2,1},{3,2},{4,7},{5,4},{6,5},{7,6},{8,11},{9,8},{10,9... | collective-permute-start | bytes 786440 | tf_op jit(solution)/shard_map/ppermute | solution.py:44
  33.8 19.1 %collective-permute-start.2 = (bf16[256,512]{1,0:T(8,128)(2,1)S(1)}, bf16[256,512]{1,0:T(8,128)(2,1)S(1)}, u32[]{:S(2)}, u32[]{:S(2)}) collective-permute-start(bf16[256,512]{1,0:T(8,128)(2,1)S(1)} %get-tuple-element.104), channel_id=1, source_target_pairs={{0,1},{1,2},{2,3},{3,0},{4,5},{5,6},{6,7},{7,4},{8,9},{9,10},{10,1... | collective-permute-start | bytes 786440 | tf_op jit(solution)/shard_map/ppermute | solution.py:44
  41.3 11.7 %collective-permute-start.5 = (bf16[256,512]{1,0:T(8,128)(2,1)S(1)}, bf16[256,512]{1,0:T(8,128)(2,1)S(1)}, u32[]{:S(2)}, u32[]{:S(2)}) collective-permute-start(bf16[256,512]{1,0:T(8,128)(2,1)S(1)} %get-tuple-element.102), channel_id=1, source_target_pairs={{0,3},{1,0},{2,1},{3,2},{4,7},{5,4},{6,5},{7,6},{8,11},{9,8},{10,9... | collective-permute-start | bytes 786440 | tf_op jit(solution)/shard_map/ppermute | solution.py:44
  54.7 4.8 %collective-permute-start.8 = (bf16[4,128,128]{2,1,0:T(8,128)(2,1)S(1)}, bf16[4,128,128]{2,1,0:T(8,128)(2,1)S(1)}, u32[]{:S(2)}, u32[]{:S(2)}) collective-permute-start(bf16[4,128,128]{2,1,0:T(8,128)(2,1)S(1)} %get-tuple-element.76), channel_id=1, source_target_pairs={{0,4},{4,0},{8,12},{12,8},{16,20},{20,16},{24,28},{28,24},{32,36},... | collective-permute-start | bytes 393224 | tf_op jit(solution)/shard_map/ppermute | solution.py:44
  59.5 5.7 %collective-permute-start.10 = (bf16[4,128,128]{2,1,0:T(8,128)(2,1)S(1)}, bf16[4,128,128]{2,1,0:T(8,128)(2,1)S(1)}, u32[]{:S(2)}, u32[]{:S(2)}) collective-permute-start(bf16[4,128,128]{2,1,0:T(8,128)(2,1)S(1)} %fusion.6), channel_id=1, source_target_pairs={{0,64},{4,20},{8,72},{12,28},{16,80},{20,4},{24,88},{28,12},{32,96... | collective-permute-start | bytes 393224 | tf_op jit(solution)/shard_map/ppermute | solution.py:44
  62.3 4.4 %collective-permute-start.11 = (bf16[4,128,128]{2,1,0:T(8,128)(2,1)S(1)}, bf16[4,128,128]{2,1,0:T(8,128)(2,1)S(1)}, u32[]{:S(2)}, u32[]{:S(2)}) collective-permute-start(bf16[4,128,128]{2,1,0:T(8,128)(2,1)S(1)} %fusion.6), channel_id=1, source_target_pairs={{0,96},{4,28},{8,104},{12,4},{16,112},{20,12},{24,120},{28,20},{32... | collective-permute-start | bytes 393224 | tf_op jit(solution)/shard_map/ppermute | solution.py:44
  63.2 5.3 %collective-permute-start.9 = (bf16[4,128,128]{2,1,0:T(8,128)(2,1)S(1)}, bf16[4,128,128]{2,1,0:T(8,128)(2,1)S(1)}, u32[]{:S(2)}, u32[]{:S(2)}) collective-permute-start(bf16[4,128,128]{2,1,0:T(8,128)(2,1)S(1)} %fusion.6), channel_id=1, source_target_pairs={{0,32},{4,12},{8,40},{12,20},{16,48},{20,28},{24,56},{28,4},{32,64... | collective-permute-start | bytes 393224 | tf_op jit(solution)/shard_map/ppermute | solution.py:44
  68.7 10.9 %collective-permute-start.12 = (bf16[4,128,128]{2,1,0:T(8,128)(2,1)S(1)}, bf16[4,128,128]{2,1,0:T(8,128)(2,1)S(1)}, u32[]{:S(2)}, u32[]{:S(2)}) collective-permute-start(bf16[4,128,128]{2,1,0:T(8,128)(2,1)S(1)} %get-tuple-element.99), channel_id=1, source_target_pairs={{0,8},{4,36},{8,16},{12,44},{16,24},{20,52},{24,0},{28,60},{32,40}... | collective-permute-start | bytes 393224 | tf_op jit(solution)/shard_map/ppermute | solution.py:44
  69.8 9.8 %collective-permute-start.13 = (bf16[4,128,128]{2,1,0:T(8,128)(2,1)S(1)}, bf16[4,128,128]{2,1,0:T(8,128)(2,1)S(1)}, u32[]{:S(2)}, u32[]{:S(2)}) collective-permute-start(bf16[4,128,128]{2,1,0:T(8,128)(2,1)S(1)} %get-tuple-element.100), channel_id=1, source_target_pairs={{0,16},{4,68},{8,24},{12,76},{16,0},{20,84},{24,8},{28,92},{32,48}... | collective-permute-start | bytes 393224 | tf_op jit(solution)/shard_map/ppermute | solution.py:44
  72.4 7.2 %collective-permute-start.14 = (bf16[4,128,128]{2,1,0:T(8,128)(2,1)S(1)}, bf16[4,128,128]{2,1,0:T(8,128)(2,1)S(1)}, u32[]{:S(2)}, u32[]{:S(2)}) collective-permute-start(bf16[4,128,128]{2,1,0:T(8,128)(2,1)S(1)} %get-tuple-element.101), channel_id=1, source_target_pairs={{0,24},{4,100},{8,0},{12,108},{16,8},{20,116},{24,16},{28,124},{32... | collective-permute-start | bytes 393224 | tf_op jit(solution)/shard_map/ppermute | solution.py:44
  77.4 6.0 %copy-start = (f32[1024]{0:T(1024)S(1)}, f32[1024]{0:T(1024)}, u32[]{:S(2)}) copy-start(f32[1024]{0:T(1024)} %param.12) | copy-start | bytes 12292
  79.8 3.6 %collective-permute-start.15 = (bf16[4,128,128]{2,1,0:T(8,128)(2,1)S(1)}, bf16[4,128,128]{2,1,0:T(8,128)(2,1)S(1)}, u32[]{:S(2)}, u32[]{:S(2)}) collective-permute-start(bf16[4,128,128]{2,1,0:T(8,128)(2,1)S(1)} %get-tuple-element.97), channel_id=1, source_target_pairs={{0,4},{4,0},{8,12},{12,8},{16,20},{20,16},{24,28},{28,24},{32,36},... | collective-permute-start | bytes 393224 | tf_op jit(solution)/shard_map/ppermute | solution.py:44
  85.6 14.4 %collective-permute-start.20 = (bf16[128,2048]{1,0:T(8,128)(2,1)S(1)}, bf16[128,2048]{1,0:T(8,128)(2,1)S(1)}, u32[]{:S(2)}, u32[]{:S(2)}) collective-permute-start(bf16[128,2048]{1,0:T(8,128)(2,1)S(1)} %get-tuple-element.96), channel_id=1, source_target_pairs={{0,1},{1,2},{2,3},{3,0},{4,5},{5,6},{6,7},{7,4},{8,9},{9,10},{10,1... | collective-permute-start | bytes 1572872 | tf_op jit(solution)/shard_map/ppermute | solution.py:44
  89.6 32.1 %collective-permute-start.19 = (bf16[128,2048]{1,0:T(8,128)(2,1)S(1)}, bf16[128,2048]{1,0:T(8,128)(2,1)S(1)}, u32[]{:S(2)}, u32[]{:S(2)}) collective-permute-start(bf16[128,2048]{1,0:T(8,128)(2,1)S(1)} %get-tuple-element.94), channel_id=1, source_target_pairs={{0,3},{1,0},{2,1},{3,2},{4,7},{5,4},{6,5},{7,6},{8,11},{9,8},{10,9... | collective-permute-start | bytes 1572872 | tf_op jit(solution)/shard_map/ppermute | solution.py:44
  93.5 20.6 %collective-permute-start.17 = (bf16[128,2048]{1,0:T(8,128)(2,1)S(1)}, bf16[128,2048]{1,0:T(8,128)(2,1)S(1)}, u32[]{:S(2)}, u32[]{:S(2)}) collective-permute-start(bf16[128,2048]{1,0:T(8,128)(2,1)S(1)} %shard_map.87), channel_id=1, source_target_pairs={{0,3},{1,0},{2,1},{3,2},{4,7},{5,4},{6,5},{7,6},{8,11},{9,8},{10,9... | collective-permute-start | bytes 1572872 | tf_op jit(solution)/shard_map/ppermute | solution.py:44
  97.5 26.0 %collective-permute-start.16 = (bf16[128,2048]{1,0:T(8,128)(2,1)S(1)}, bf16[128,2048]{1,0:T(8,128)(2,1)S(1)}, u32[]{:S(2)}, u32[]{:S(2)}) collective-permute-start(bf16[128,2048]{1,0:T(8,128)(2,1)S(1)} %get-tuple-element.90), channel_id=1, source_target_pairs={{0,1},{1,2},{2,3},{3,0},{4,5},{5,6},{6,7},{7,4},{8,9},{9,10},{10,1... | collective-permute-start | bytes 1572872 | tf_op jit(solution)/shard_map/ppermute | solution.py:44
  100.1 22.4 %collective-permute-start.21 = (bf16[128,2048]{1,0:T(8,128)(2,1)S(1)}, bf16[128,2048]{1,0:T(8,128)(2,1)S(1)}, u32[]{:S(2)}, u32[]{:S(2)}) collective-permute-start(bf16[128,2048]{1,0:T(8,128)(2,1)S(1)} %add_convert_fusion), channel_id=1, source_target_pairs={{0,1},{1,2},{2,3},{3,0},{4,5},{5,6},{6,7},{7,4},{8,9},{9,10},{10,1... | collective-permute-start | bytes 1572872 | tf_op jit(solution)/shard_map/ppermute | solution.py:44
  114.3 13.3 %collective-permute-start.18 = (bf16[128,2048]{1,0:T(8,128)(2,1)S(1)}, bf16[128,2048]{1,0:T(8,128)(2,1)S(1)}, u32[]{:S(2)}, u32[]{:S(2)}) collective-permute-start(bf16[128,2048]{1,0:T(8,128)(2,1)S(1)} %add_convert_fusion.1), channel_id=1, source_target_pairs={{0,3},{1,0},{2,1},{3,2},{4,7},{5,4},{6,5},{7,6},{8,11},{9,8},{10,9... | collective-permute-start | bytes 1572872 | tf_op jit(solution)/shard_map/ppermute | solution.py:44
